TPU v7x, 32 devices: a whole 2x2x4 slice. The times are simulated.
32 devices in a mesh: ctx: 4 (over y, core), fsdp: 8 (over z, x).
Axes of the slice: x: 2, y: 2, z: 4, core: 2. Of those that a mesh axis runs over, the one named last changes fastest.
Arguments:
- inputs: bfloat16 [8, 512, 2048], P('fsdp', 'ctx'), may hold values from -6 to 6
- lengths: int32 [8], P('fsdp'), may hold values from 256 to 512, as said below
- norm1_gain: bfloat16 [2048], P('fsdp'), may hold values from 0.5 to 1.5
- norm1_bias: bfloat16 [2048], P('fsdp'), may hold values from -1.25 to 1.25
- query_weight: bfloat16 [2048, 2048], P('fsdp'), may hold values from -3 to 3, as said below
- query_bias: bfloat16 [2048], P('fsdp'), may hold values from -3 to 3
- keyval_weight: bfloat16 [2048, 256], P('fsdp'), may hold values from -0.125 to 0.125
- value_bias: bfloat16 [128], P('fsdp'), may hold values from -3 to 3
- output_weight: bfloat16 [2048, 2048], P('fsdp'), may hold values from -0.75 to 0.75
- output_bias: bfloat16 [2048], P('fsdp'), may hold values from -3 to 3
- norm2_gain: bfloat16 [2048], P('fsdp'), may hold values from 0.5 to 1.5
- norm2_bias: bfloat16 [2048], P('fsdp'), may hold values from -1.25 to 1.25
- up_weight: bfloat16 [2048, 8192], P('fsdp'), may hold values from -0.125 to 0.125
- up_bias: bfloat16 [8192], P('fsdp'), may hold values from -3 to 3
- down_weight: bfloat16 [8192, 2048], P('fsdp'), may hold values from -0.0625 to 0.0625
- down_bias: bfloat16 [2048], P('fsdp'), may hold values from -3 to 3
- cotangent: bfloat16 [8, 512, 2048], P('fsdp', 'ctx'), may hold values from -6 to 6
Outputs:
- result: bfloat16 [8, 512, 2048], P('fsdp', 'ctx')
- input_grad: bfloat16 [8, 512, 2048], P('fsdp', 'ctx')
- grad_norm1_gain: float32 [2048], P('fsdp')
- grad_norm1_bias: float32 [2048], P('fsdp')
- grad_query_weight: float32 [2048, 2048], P('fsdp')
- grad_query_bias: float32 [2048], P('fsdp')
- grad_keyval_weight: float32 [2048, 256], P('fsdp')
- grad_value_bias: float32 [128], P('fsdp')
- grad_output_weight: float32 [2048, 2048], P('fsdp')
- grad_output_bias: float32 [2048], P('fsdp')
- grad_norm2_gain: float32 [2048], P('fsdp')
- grad_norm2_bias: float32 [2048], P('fsdp')
- grad_up_weight: float32 [2048, 8192], P('fsdp')
- grad_up_bias: float32 [8192], P('fsdp')
- grad_down_weight: float32 [8192, 2048], P('fsdp')
- grad_down_bias: float32 [2048], P('fsdp')
- clipped_query_weight: bfloat16 [2048, 2048], P('fsdp')
- clipped_query_bias: bfloat16 [2048], P('fsdp')
- clipped_keyval_weight: bfloat16 [2048, 256], P('fsdp')
Inputs may be any that keep to these rules, and one draw needn't show every extreme that they name: Sequence b's live tokens are its first lengths[b]; in every draw some sequence is live over all 512 tokens. `query_weight`: a dense matrix.
All inputs are finite; a program needn't handle non-finite values.
Results may differ from a plain program's by a relative error of at most 0.019.
Values may be sent and summed in bfloat16 or wider, within the bound.
A program may use at most 384 MiB of HBM per device.

v0:
```python
import jax
import jax.numpy as jnp
from jax import lax
from jax.sharding import PartitionSpec as P

H = 16
HD = 128


EPSILON = 1e-05
CLIP_LIMIT = 10.0
NEGATIVE = -1e30


def layer_norm(values, gain, shift):
    center = values - jnp.mean(values, -1, keepdims=True)
    spread = jnp.mean(center * center, -1, keepdims=True)
    return center * lax.rsqrt(spread + EPSILON) * gain + shift


def gelu_tanh(values):
    return jax.nn.gelu(values, approximate=True)


def matmul(left, right):
    return jnp.dot(left, right, preferred_element_type=jnp.float32)


def matmul_tn(left, right):
    return lax.dot_general(
        left, right, (((0,), (0,)), ((), ())), preferred_element_type=jnp.float32
    )


def matmul_nt(left, right):
    return lax.dot_general(
        left, right, (((1,), (1,)), ((), ())), preferred_element_type=jnp.float32
    )


def column_sum(values):
    return jnp.sum(values.astype(jnp.float32), 0)


def body(
    inputs,
    lengths,
    norm1_gain,
    norm1_bias,
    query_weight,
    query_bias,
    keyval_weight,
    value_bias,
    output_weight,
    output_bias,
    norm2_gain,
    norm2_bias,
    up_weight,
    up_bias,
    down_weight,
    down_bias,
    cotangent,
):
    local_rows = inputs.shape[1]
    width = inputs.shape[2]
    ctx_count = lax.axis_size("ctx")
    ctx_index = lax.axis_index("ctx")
    shard_index = lax.axis_index("fsdp")
    head_rows = H * local_rows
    scale = HD ** (-0.5)
    length = lengths[0]
    attn_parts = (
        lax.all_gather(norm1_gain, "fsdp", axis=0, tiled=True),
        lax.all_gather(norm1_bias, "fsdp", axis=0, tiled=True),
        lax.all_gather(query_weight, "fsdp", axis=0, tiled=True),
        lax.all_gather(query_bias, "fsdp", axis=0, tiled=True),
        lax.all_gather(keyval_weight, "fsdp", axis=0, tiled=True),
        lax.all_gather(value_bias, "fsdp", axis=0, tiled=True),
        lax.all_gather(output_weight, "fsdp", axis=0, tiled=True),
        lax.all_gather(output_bias, "fsdp", axis=0, tiled=True),
    )
    (
        whole_gain_one,
        whole_shift_one,
        whole_query,
        whole_query_bias,
        whole_keyval,
        whole_value_bias,
        whole_output,
        whole_output_bias,
    ) = attn_parts
    rows_in = inputs[0].astype(jnp.float32)
    gain_one = whole_gain_one.astype(jnp.float32)
    shift_one = whole_shift_one.astype(jnp.float32)
    normed = layer_norm(rows_in, gain_one, shift_one)
    normed_low = normed.astype(jnp.bfloat16)
    queries = (matmul(normed_low, whole_query) + whole_query_bias.astype(jnp.float32)).astype(
        jnp.bfloat16
    )
    value_shift = jnp.concatenate(
        [jnp.zeros((HD,), jnp.float32), whole_value_bias.astype(jnp.float32)]
    )
    keyvals = (matmul(normed_low, whole_keyval) + value_shift).astype(jnp.bfloat16)
    all_keyvals = lax.all_gather(keyvals, "ctx", axis=0, tiled=True)
    query_rows = queries.reshape(local_rows, H, HD).transpose(1, 0, 2).reshape(head_rows, HD)
    positions = ctx_index * local_rows + jnp.arange(local_rows, dtype=jnp.int32)
    row_positions = jnp.tile(positions, H)
    live_rows = (positions < length).astype(jnp.float32)

    def block_scores(block_index):
        first_row = block_index * local_rows
        block_keys = lax.dynamic_slice_in_dim(all_keyvals, first_row, local_rows, 0)
        raw_scores = matmul_nt(query_rows, block_keys[:, :HD]) * scale
        key_positions = first_row + jnp.arange(local_rows, dtype=jnp.int32)
        allowed = (key_positions[None, :] <= row_positions[:, None]) & (
            key_positions[None, :] < length
        )
        return (raw_scores, allowed, block_keys)

    def active(block_index):
        return (block_index <= ctx_index) & (block_index * local_rows < length)

    def stats_step(block_index, carried):

        def stats_work(current):
            run_max, run_sum = current
            raw_scores, allowed, block_keys = block_scores(block_index)
            masked = jnp.where(allowed, raw_scores, NEGATIVE)
            new_max = jnp.maximum(run_max, jnp.max(masked, 1))
            summands = jnp.where(allowed, jnp.exp(masked - new_max[:, None]), 0.0)
            return (new_max, run_sum * jnp.exp(run_max - new_max) + jnp.sum(summands, 1))

        return lax.cond(active(block_index), stats_work, lambda current: current, carried)

    start_state = (
        jnp.full((head_rows,), NEGATIVE, jnp.float32),
        jnp.zeros((head_rows,), jnp.float32),
    )
    row_max, row_sum = lax.fori_loop(0, ctx_count, stats_step, start_state)
    log_total = row_max + jnp.log(row_sum)
    head_top = jnp.max(
        jnp.where(live_rows[None, :] > 0, row_max.reshape(H, local_rows), NEGATIVE), 1
    )
    top_logit = lax.pmax(head_top, ("ctx", "fsdp"))

    def output_step(block_index, carried):

        def output_work(totals):
            raw_scores, allowed, block_keys = block_scores(block_index)
            weights = jnp.where(allowed, jnp.exp(raw_scores - log_total[:, None]), 0.0).astype(
                jnp.bfloat16
            )
            return totals + matmul(weights, block_keys[:, HD:])

        return lax.cond(active(block_index), output_work, lambda totals: totals, carried)

    attended_rows = lax.fori_loop(
        0, ctx_count, output_step, jnp.zeros((head_rows, HD), jnp.float32)
    )
    attended = (
        attended_rows.reshape(H, local_rows, HD).transpose(1, 0, 2).reshape(local_rows, width)
    )
    attended = attended.astype(jnp.bfloat16)
    mlp_parts = (
        lax.all_gather(norm2_gain, "fsdp", axis=0, tiled=True),
        lax.all_gather(norm2_bias, "fsdp", axis=0, tiled=True),
        lax.all_gather(up_weight, "fsdp", axis=0, tiled=True),
        lax.all_gather(up_bias, "fsdp", axis=0, tiled=True),
        lax.all_gather(down_weight, "fsdp", axis=0, tiled=True),
        lax.all_gather(down_bias, "fsdp", axis=0, tiled=True),
    )
    whole_gain_two, whole_shift_two, whole_up, whole_up_bias, whole_down, whole_down_bias = (
        mlp_parts
    )
    middle = rows_in + matmul(attended, whole_output) + whole_output_bias.astype(jnp.float32)
    gain_two = whole_gain_two.astype(jnp.float32)
    shift_two = whole_shift_two.astype(jnp.float32)
    normed_two = layer_norm(middle, gain_two, shift_two).astype(jnp.bfloat16)
    pre_act = matmul(normed_two, whole_up) + whole_up_bias.astype(jnp.float32)
    act_low = gelu_tanh(pre_act).astype(jnp.bfloat16)
    mlp_out = matmul(act_low, whole_down) + whole_down_bias.astype(jnp.float32)
    result = (live_rows[:, None] * (middle + mlp_out)).astype(jnp.bfloat16)[None]
    grad_out = live_rows[:, None] * cotangent[0].astype(jnp.float32)
    grad_mlp = grad_out.astype(jnp.bfloat16)
    grad_down_bias = column_sum(grad_mlp)
    grad_act = matmul_nt(grad_mlp, whole_down)
    unused_gelu, gelu_back = jax.vjp(gelu_tanh, pre_act)
    grad_pre = gelu_back(grad_act)[0].astype(jnp.bfloat16)
    grad_up_bias = column_sum(grad_pre)
    down_piece = lax.psum_scatter(
        matmul_tn(act_low, grad_mlp).astype(jnp.bfloat16), "fsdp", scatter_dimension=0, tiled=True
    )
    up_piece = lax.psum_scatter(
        matmul_tn(normed_two, grad_pre).astype(jnp.bfloat16),
        "fsdp",
        scatter_dimension=0,
        tiled=True,
    )
    grad_two = matmul_nt(grad_pre, whole_up)
    unused_norm, norm_back_two = jax.vjp(layer_norm, middle, gain_two, shift_two)
    grad_middle_part, grad_gain_two, grad_shift_two = norm_back_two(grad_two)
    grad_middle = grad_out + grad_middle_part
    grad_branch = grad_middle.astype(jnp.bfloat16)
    grad_output_bias = column_sum(grad_branch)
    grad_att = matmul_nt(grad_branch, whole_output).astype(jnp.bfloat16)
    grad_att_rows = grad_att.reshape(local_rows, H, HD).transpose(1, 0, 2).reshape(head_rows, HD)

    def delta_step(block_index, carried):

        def delta_work(totals):
            raw_scores, allowed, block_keys = block_scores(block_index)
            weights = jnp.where(allowed, jnp.exp(raw_scores - log_total[:, None]), 0.0)
            grad_weights = matmul_nt(grad_att_rows, block_keys[:, HD:])
            return totals + jnp.sum(weights * grad_weights, 1)

        return lax.cond(active(block_index), delta_work, lambda totals: totals, carried)

    delta = lax.fori_loop(0, ctx_count, delta_step, jnp.zeros((head_rows,), jnp.float32))

    def grad_step(block_index, carried):

        def grad_work(current):
            grad_query_rows, grad_keyvals_all = current
            raw_scores, allowed, block_keys = block_scores(block_index)
            weights = jnp.where(allowed, jnp.exp(raw_scores - log_total[:, None]), 0.0)
            grad_weights = matmul_nt(grad_att_rows, block_keys[:, HD:])
            grad_scores = (weights * (grad_weights - delta[:, None])).astype(jnp.bfloat16)
            grad_query_rows = grad_query_rows + matmul(grad_scores, block_keys[:, :HD])
            grad_keys = matmul_tn(grad_scores, query_rows) * scale
            grad_values = matmul_tn(weights.astype(jnp.bfloat16), grad_att_rows)
            update = jnp.concatenate([grad_keys, grad_values], 1)
            grad_keyvals_all = lax.dynamic_update_slice_in_dim(
                grad_keyvals_all, update, block_index * local_rows, 0
            )
            return (grad_query_rows, grad_keyvals_all)

        return lax.cond(active(block_index), grad_work, lambda current: current, carried)

    grad_start = (
        jnp.zeros((head_rows, HD), jnp.float32),
        jnp.zeros((ctx_count * local_rows, 2 * HD), jnp.float32),
    )
    grad_query_rows, grad_keyvals_all = lax.fori_loop(0, ctx_count, grad_step, grad_start)
    grad_keyvals_own = lax.psum_scatter(
        grad_keyvals_all.astype(jnp.bfloat16), "ctx", scatter_dimension=0, tiled=True
    )
    grad_queries = (grad_query_rows * scale).reshape(H, local_rows, HD).transpose(1, 0, 2)
    grad_queries = grad_queries.reshape(local_rows, width).astype(jnp.bfloat16)
    grad_query_bias = column_sum(grad_queries)
    grad_value_bias = column_sum(grad_keyvals_own[:, HD:])
    grad_one = matmul_nt(grad_queries, whole_query) + matmul_nt(grad_keyvals_own, whole_keyval)
    unused_first, norm_back_one = jax.vjp(layer_norm, rows_in, gain_one, shift_one)
    grad_in_part, grad_gain_one, grad_shift_one = norm_back_one(grad_one)
    input_grad = (grad_middle + grad_in_part).astype(jnp.bfloat16)[None]
    grad_query_weight = matmul_tn(normed_low, grad_queries)
    grad_keyval_weight = matmul_tn(normed_low, grad_keyvals_own)
    grad_output_weight = matmul_tn(attended, grad_branch)
    shards = (
        lax.psum_scatter(
            grad_gain_one.astype(jnp.bfloat16), "fsdp", scatter_dimension=0, tiled=True
        ).astype(jnp.float32),
        lax.psum_scatter(
            grad_shift_one.astype(jnp.bfloat16), "fsdp", scatter_dimension=0, tiled=True
        ).astype(jnp.float32),
        lax.psum_scatter(
            grad_query_weight.astype(jnp.bfloat16), "fsdp", scatter_dimension=0, tiled=True
        ).astype(jnp.float32),
        lax.psum_scatter(
            grad_query_bias.astype(jnp.bfloat16), "fsdp", scatter_dimension=0, tiled=True
        ).astype(jnp.float32),
        lax.psum_scatter(
            grad_keyval_weight.astype(jnp.bfloat16), "fsdp", scatter_dimension=0, tiled=True
        ).astype(jnp.float32),
        lax.psum_scatter(
            grad_value_bias.astype(jnp.bfloat16), "fsdp", scatter_dimension=0, tiled=True
        ).astype(jnp.float32),
        lax.psum_scatter(
            grad_output_weight.astype(jnp.bfloat16), "fsdp", scatter_dimension=0, tiled=True
        ).astype(jnp.float32),
        lax.psum_scatter(
            grad_output_bias.astype(jnp.bfloat16), "fsdp", scatter_dimension=0, tiled=True
        ).astype(jnp.float32),
        lax.psum_scatter(
            grad_gain_two.astype(jnp.bfloat16), "fsdp", scatter_dimension=0, tiled=True
        ).astype(jnp.float32),
        lax.psum_scatter(
            grad_shift_two.astype(jnp.bfloat16), "fsdp", scatter_dimension=0, tiled=True
        ).astype(jnp.float32),
        lax.psum_scatter(
            grad_up_bias.astype(jnp.bfloat16), "fsdp", scatter_dimension=0, tiled=True
        ).astype(jnp.float32),
        lax.psum_scatter(
            grad_down_bias.astype(jnp.bfloat16), "fsdp", scatter_dimension=0, tiled=True
        ).astype(jnp.float32),
    )
    (
        shard_gain_one,
        shard_shift_one,
        shard_query_weight,
        shard_query_bias,
        shard_keyval_weight,
        shard_value_bias,
        shard_output_weight,
        shard_output_bias,
        shard_gain_two,
        shard_shift_two,
        shard_up_bias,
        shard_down_bias,
    ) = shards
    totals = (
        lax.psum(shard_gain_one.astype(jnp.bfloat16), "ctx").astype(jnp.float32),
        lax.psum(shard_shift_one.astype(jnp.bfloat16), "ctx").astype(jnp.float32),
        lax.psum(shard_query_weight.astype(jnp.bfloat16), "ctx").astype(jnp.float32),
        lax.psum(shard_query_bias.astype(jnp.bfloat16), "ctx").astype(jnp.float32),
        lax.psum(shard_keyval_weight.astype(jnp.bfloat16), "ctx").astype(jnp.float32),
        lax.psum(shard_value_bias.astype(jnp.bfloat16), "ctx").astype(jnp.float32),
        lax.psum(shard_output_weight.astype(jnp.bfloat16), "ctx").astype(jnp.float32),
        lax.psum(shard_output_bias.astype(jnp.bfloat16), "ctx").astype(jnp.float32),
        lax.psum(shard_gain_two.astype(jnp.bfloat16), "ctx").astype(jnp.float32),
        lax.psum(shard_shift_two.astype(jnp.bfloat16), "ctx").astype(jnp.float32),
        lax.psum(up_piece, "ctx").astype(jnp.float32),
        lax.psum(shard_up_bias.astype(jnp.bfloat16), "ctx").astype(jnp.float32),
        lax.psum(down_piece, "ctx").astype(jnp.float32),
        lax.psum(shard_down_bias.astype(jnp.bfloat16), "ctx").astype(jnp.float32),
    )
    factors = CLIP_LIMIT / jnp.maximum(top_logit, CLIP_LIMIT)
    column_scale = jnp.repeat(jnp.sqrt(factors), HD)
    rows_here = query_weight.shape[0]
    clipped_query_weight = (query_weight.astype(jnp.float32) * column_scale[None, :]).astype(
        jnp.bfloat16
    )
    bias_scale = lax.dynamic_slice_in_dim(column_scale, shard_index * rows_here, rows_here, 0)
    clipped_query_bias = (query_bias.astype(jnp.float32) * bias_scale).astype(jnp.bfloat16)
    key_scale = jnp.sqrt(jnp.min(factors))
    keyval_scale = jnp.concatenate(
        [jnp.full((HD,), 1.0, jnp.float32) * key_scale, jnp.ones((HD,), jnp.float32)]
    )
    clipped_keyval_weight = (keyval_weight.astype(jnp.float32) * keyval_scale[None, :]).astype(
        jnp.bfloat16
    )
    return (
        result,
        input_grad,
        totals[0],
        totals[1],
        totals[2],
        totals[3],
        totals[4],
        totals[5],
        totals[6],
        totals[7],
        totals[8],
        totals[9],
        totals[10],
        totals[11],
        totals[12],
        totals[13],
        clipped_query_weight,
        clipped_query_bias,
        clipped_keyval_weight,
    )


def solution(mesh):
    return jax.shard_map(
        body,
        mesh=mesh,
        in_specs=(
            P("fsdp", "ctx", None),
            P("fsdp"),
            P("fsdp"),
            P("fsdp"),
            P("fsdp", None),
            P("fsdp"),
            P("fsdp", None),
            P("fsdp"),
            P("fsdp", None),
            P("fsdp"),
            P("fsdp"),
            P("fsdp"),
            P("fsdp", None),
            P("fsdp"),
            P("fsdp", None),
            P("fsdp"),
            P("fsdp", "ctx", None),
        ),
        out_specs=(
            P("fsdp", "ctx", None),
            P("fsdp", "ctx", None),
            P("fsdp"),
            P("fsdp"),
            P("fsdp", None),
            P("fsdp"),
            P("fsdp", None),
            P("fsdp"),
            P("fsdp", None),
            P("fsdp"),
            P("fsdp"),
            P("fsdp"),
            P("fsdp", None),
            P("fsdp"),
            P("fsdp", None),
            P("fsdp"),
            P("fsdp", None),
            P("fsdp"),
            P("fsdp", None),
        ),
        check_vma=False,
    )
```

profile of v0, /device:TPU:0, one launch (start us, length us, event | category | flops | bytes accessed | tf_op | source)
XLA Modules:
  0.0 3353.4 jit_solution(1405585250045505267)
XLA Ops:
  10.8 22.2 all-gather.3
  33.1 16.3 all-gather.1
  49.4 18.3 all-gather
  67.7 16.7 all-gather.2
  85.0 26.3 all_gather.57
  111.4 16.9 all-gather.5
  128.4 18.1 all-gather.4
  148.0 18.2 all-reduce.2
  174.1 5.9 all-gather.15.cloned.1.call-done
  194.2 111.1 %all-gather.17.cloned.1.call-done = bf16[2048,2048]{1,0:T(8,128)(2,1)} async-done(((bf16[256,2048]{1,0:T(8,128)(2,1)}), bf16[2048,2048]{1,0:T(8,128)(2,1)}) %all-gather.17.cloned.1.call-update) | async-done | bytes 8388624 | tf_op jit(solution)/shard_map/all_gather | solution.py:79
  310.3 632.3 %all-gather.19.cloned.1.call-done = bf16[2048,8192]{1,0:T(8,128)(2,1)} async-done(((bf16[256,8192]{1,0:T(8,128)(2,1)}), bf16[2048,8192]{1,0:T(8,128)(2,1)}) %all-gather.19.cloned.1.call-update) | async-done | bytes 33554448 | tf_op jit(solution)/shard_map/all_gather | solution.py:167
  942.6 18.2 convolution_add_fusion.2
  960.8 620.9 %all-gather.21.cloned.1.call-done = bf16[8192,2048]{1,0:T(8,128)(2,1)} async-done(((bf16[1024,2048]{1,0:T(8,128)(2,1)}), bf16[8192,2048]{1,0:T(8,128)(2,1)}) %all-gather.21.cloned.1.call-update) | async-done | bytes 33554448 | tf_op jit(solution)/shard_map/all_gather | solution.py:169
  1581.7 19.0 fusion.118
  1600.7 16.8 multiply_reduce_fusion
  1619.2 6.5 fusion.74
  1631.1 5.9 while.69
  1639.0 33.8 %reduce-scatter.19.cloned.1.call-done = bf16[128,256]{1,0:T(8,128)(2,1)} async-done(((bf16[512,256]{1,0:T(8,128)(2,1)}), bf16[128,256]{1,0:T(8,128)(2,1)}) %reduce-scatter.19.cloned.1.call-update) | async-done | bytes 65552
  1675.9 5.9 convolution_convert_fusion.3
  1689.9 15.4 convolution_convert_fusion
  1706.4 16.2 convolution_convert_fusion.1
  1723.3 20.4 all-gather.6
  1745.8 41.4 %pmax.7 = f32[16]{0:T(128)S(1)} all-reduce(f32[16]{0:T(128)S(1)} %fusion.97), channel_id=1, replica_groups=mesh['ctx'=4,'fsdp'=8] {'ctx','fsdp'}, use_global_device_ids=true, to_apply=%region_66.67 | all-reduce | flops 16 | bytes 128 | tf_op jit(solution)/shard_map/pmax | solution.py:144
  1788.6 104.6 %reduce-scatter.9.cloned.1.call-done = bf16[256,2048]{1,0:T(8,128)(2,1)} async-done(((bf16[2048,2048]{1,0:T(8,128)(2,1)}), bf16[256,2048]{1,0:T(8,128)(2,1)}) %reduce-scatter.9.cloned.1.call-update) | async-done | bytes 1048592 | tf_op jit(solution)/shard_map/reduce_scatter | solution.py:265
  1893.2 152.7 %reduce-scatter.13.cloned.1.call-done = bf16[256,2048]{1,0:T(8,128)(2,1)} async-done(((bf16[2048,2048]{1,0:T(8,128)(2,1)}), bf16[256,2048]{1,0:T(8,128)(2,1)}) %reduce-scatter.13.cloned.1.call-update) | async-done | bytes 1048592 | tf_op jit(solution)/shard_map/reduce_scatter | solution.py:277
  2045.9 545.7 %reduce-scatter.15.cloned.1.call-done = bf16[256,8192]{1,0:T(8,128)(2,1)} async-done(((bf16[2048,8192]{1,0:T(8,128)(2,1)}), bf16[256,8192]{1,0:T(8,128)(2,1)}) %reduce-scatter.15.cloned.1.call-update) | async-done | bytes 4194320 | tf_op jit(solution)/shard_map/reduce_scatter | solution.py:193
  2591.6 546.1 %reduce-scatter.17.cloned.1.call-done = bf16[1024,2048]{1,0:T(8,128)(2,1)} async-done(((bf16[8192,2048]{1,0:T(8,128)(2,1)}), bf16[1024,2048]{1,0:T(8,128)(2,1)}) %reduce-scatter.17.cloned.1.call-update) | async-done | bytes 4194320 | tf_op jit(solution)/shard_map/reduce_scatter | solution.py:190
  3142.0 6.7 fusion.119
  3148.7 18.1 fusion.67
  3169.4 35.3 %all-reduce.12 = (bf16[2048]{0:T(1024)(128)(2,1)S(1)}, bf16[2048]{0:T(1024)(128)(2,1)S(1)}, bf16[2048]{0:T(1024)(128)(2,1)S(1)}, bf16[128]{0:T(256)(128)(2,1)S(1...) all-reduce(bf16[2048]{0:T(1024)(128)(2,1)S(1)} %get-tuple-element.8, ...), channel_id=3, replica_groups=mesh['ctx'=4,'fsdp'=8] {'fsdp'}, use_global_device_ids=true, to_apply=%region_29.30.clone | all-reduce | flops 22656 | bytes 90624
  3205.3 6.8 all-reduce.13
  3218.5 111.7 %all-reduce.17.cloned.1.call-done = (bf16[256,2048]{1,0:T(8,128)(2,1)}, bf16[256,256]{1,0:T(8,128)(2,1)}, bf16[256,2048]{1,0:T(8,128)(2,1)}, bf16[256,8192]{1,0:T(8,128)(2,1)}, bf16[1024,2048]{1,0:T(8,128)(2,1)}) async-done(((bf16[256,2048]{1,0:T(8,128)(2,1)}, bf16[256,256]{1,0:T(8,128)(2,1)}, bf16[256,2048]{1,0:T(8,128)(2,1)}, bf16[256,8192]{1,0:T(8,128)(2,1)}, bf16[1024,2048]{1,0:T(8,128)(2,1)}), ...) | async-done | bytes 10616848 | tf_op jit(solution)/shard_map/psum | solution.py:313
  (222 shorter events, 99.3 us)
Async XLA Ops:
  7.2 159.5 %all-gather.13.cloned.1.call-start = ((), (), s32[]{:S(2)}) async-start(), calls=%async_computation.6 | async-start | bytes 1179648 | tf_op jit(solution)/shard_map/all_gather | solution.py:77
  7.9 172.1 %all-gather.15.cloned.1.call-start = ((), (), s32[]{:S(2)}) async-start(), calls=%async_computation.7 | async-start | bytes 9437184 | tf_op jit(solution)/shard_map/all_gather | solution.py:75
  8.7 296.6 %all-gather.17.cloned.1.call-start = ((), (), s32[]{:S(2)}) async-start(), calls=%async_computation.8 | async-start | bytes 9437184 | tf_op jit(solution)/shard_map/all_gather | solution.py:79
  9.4 23.6 copy-start.23
  9.4 40.0 %copy-start.24 = (bf16[256]{0:T(256)(128)(2,1)S(1)}, bf16[256]{0:T(256)(128)(2,1)}, u32[]{:S(2)}) copy-start(bf16[256]{0:T(256)(128)(2,1)} %param.35) | copy-start | bytes 1540
  9.4 58.2 %copy-start.18 = (bf16[256]{0:T(256)(128)(2,1)S(1)}, bf16[256]{0:T(256)(128)(2,1)}, u32[]{:S(2)}) copy-start(bf16[256]{0:T(256)(128)(2,1)} %param.38) | copy-start | bytes 1540
  9.5 75.6 %copy-start.16 = (bf16[1024]{0:T(1024)(128)(2,1)S(1)}, bf16[1024]{0:T(1024)(128)(2,1)}, u32[]{:S(2)}) copy-start(bf16[1024]{0:T(1024)(128)(2,1)} %param.46) | copy-start | bytes 6148
  9.5 101.9 %copy-start.25 = (bf16[256]{0:T(256)(128)(2,1)S(1)}, bf16[256]{0:T(256)(128)(2,1)}, u32[]{:S(2)}) copy-start(bf16[256]{0:T(256)(128)(2,1)} %param.44) | copy-start | bytes 1540
  9.5 118.9 %copy-start.26 = (bf16[256]{0:T(256)(128)(2,1)S(1)}, bf16[256]{0:T(256)(128)(2,1)}, u32[]{:S(2)}) copy-start(bf16[256]{0:T(256)(128)(2,1)} %param.43) | copy-start | bytes 1540
  9.5 137.0 %copy-start.17 = (u32[32]{0:T(128)S(1)}, u32[32]{0:T(128)}, u32[]{:S(2)}) copy-start(u32[32]{0:T(128)} %constant.186) | copy-start | bytes 388
  9.5 138.2 %copy-start.27 = (bf16[16]{0:T(256)(128)(2,1)S(1)}, bf16[16]{0:T(256)(128)(2,1)}, u32[]{:S(2)}) copy-start(bf16[16]{0:T(256)(128)(2,1)} %param.40) | copy-start | bytes 100
  9.5 156.7 %copy-start.2 = (bf16[1,128,2048]{2,1,0:T(8,128)(2,1)S(1)}, bf16[1,128,2048]{2,1,0:T(8,128)(2,1)}, u32[]{:S(2)}) copy-start(bf16[1,128,2048]{2,1,0:T(8,128)(2,1)} %param.33) | copy-start | bytes 1572868
  9.5 933.1 %all-gather.19.cloned.1.call-start = ((), (), s32[]{:S(2)}) async-start(), calls=%async_computation.9 | async-start | bytes 37748736 | tf_op jit(solution)/shard_map/all_gather | solution.py:167
  10.1 1571.6 %all-gather.21.cloned.1.call-start = ((), (), s32[]{:S(2)}) async-start(), calls=%async_computation.10 | async-start | bytes 37748736 | tf_op jit(solution)/shard_map/all_gather | solution.py:169
  10.7 1662.1 %reduce-scatter.19.cloned.1.call-start = ((), (), s32[]{:S(2)}) async-start(), calls=%async_computation.16 | async-start | bytes 327680
  166.7 18.1 copy-start.20
  194.2 115.8 %copy-start.4 = (bf16[128,16,128]{0,2,1:T(8,128)(2,1)}, bf16[128,16,128]{0,2,1:T(8,128)(2,1)S(1)}, u32[]{:S(2)}) copy-start(bf16[128,16,128]{0,2,1:T(8,128)(2,1)S(1)} %copy.49) | copy-start | bytes 1572868
  310.0 1307.5 %copy-start = (f32[128,2048]{1,0:T(8,128)}, f32[128,2048]{1,0:T(8,128)S(1)}, u32[]{:S(2)}) copy-start(f32[128,2048]{1,0:T(8,128)S(1)} %get-tuple-element.985) | copy-start | bytes 3145732
  942.6 639.1 %copy-start.8 = (bf16[1,128,2048]{2,1,0:T(8,128)(2,1)S(1)}, bf16[1,128,2048]{2,1,0:T(8,128)(2,1)}, u32[]{:S(2)}) copy-start(bf16[1,128,2048]{2,1,0:T(8,128)(2,1)} %param.49) | copy-start | bytes 1572868
  1619.2 6.5 copy-start.10
  1637.0 38.9 %copy-start.3 = (bf16[1,128,2048]{2,1,0:T(8,128)(2,1)S(1)}, bf16[1,128,2048]{2,1,0:T(8,128)(2,1)}, u32[]{:S(2)}) copy-start(bf16[1,128,2048]{2,1,0:T(8,128)(2,1)} %param.33) | copy-start | bytes 1572868
  1638.9 149.7 %reduce-scatter.11.cloned.1.call-start = ((), (), s32[]{:S(2)}) async-start(), calls=%async_computation.12 | async-start | bytes 1179648 | tf_op jit(solution)/shard_map/reduce_scatter | solution.py:271
  1675.4 217.8 %reduce-scatter.9.cloned.1.call-start = ((), (), s32[]{:S(2)}) async-start(), calls=%async_computation.11 | async-start | bytes 9437184 | tf_op jit(solution)/shard_map/reduce_scatter | solution.py:265
  1681.8 364.1 %reduce-scatter.13.cloned.1.call-start = ((), (), s32[]{:S(2)}) async-start(), calls=%async_computation.13 | async-start | bytes 9437184 | tf_op jit(solution)/shard_map/reduce_scatter | solution.py:277
  1688.7 902.9 %reduce-scatter.15.cloned.1.call-start = ((), (), s32[]{:S(2)}) async-start(), calls=%async_computation.14 | async-start | bytes 37748736 | tf_op jit(solution)/shard_map/reduce_scatter | solution.py:193
  1705.4 1432.3 %reduce-scatter.17.cloned.1.call-start = ((), (), s32[]{:S(2)}) async-start(), calls=%async_computation.15 | async-start | bytes 37748736 | tf_op jit(solution)/shard_map/reduce_scatter | solution.py:190
  1722.7 1607.5 %all-reduce.17.cloned.1.call-start = ((), (), s32[]{:S(2)}) async-start(), calls=%async_computation.17 | async-start | bytes 21233664 | tf_op jit(solution)/shard_map/psum | solution.py:313
  3148.7 18.2 copy-start.15
  3148.7 20.1 copy-start.21
  3166.9 50.3 %copy-start.7 = (f32[128,2048]{1,0:T(8,128)S(1)}, f32[128,2048]{1,0:T(8,128)}, u32[]{:S(2)}) copy-start(f32[128,2048]{1,0:T(8,128)} %copy-done.6) | copy-start | bytes 3145732
  3330.2 7.4 copy-start.13
  3337.6 4.4 copy-start.12
  (9 other events, 9.4 us)
Sparse Core Ops, SparseCore 0:
  10.2 42.9 all-gather.12
  55.3 124.6 all-gather.14
  182.1 123.0 all-gather.16
  306.7 635.9 all-gather.18
  944.0 637.6 all-gather.20
  1639.0 33.6 reduce-scatter.18
  1676.5 63.3 reduce-scatter.10
  1744.1 148.9 reduce-scatter.8
  1897.8 148.0 reduce-scatter.12
  2049.5 542.0 reduce-scatter.14
  2595.4 542.2 reduce-scatter.16
  3140.6 189.5 all-reduce.16
where the time goes:
time: 3360 us; the launch traced here: 3350 us
  waiting for transfers between devices  2870 us (85%)
  blocking collectives  263 us (8%)
  matrix products  148 us (4%)
    all_gather x1, waiting for transfers between devices, body(): lax.all_gather(up_weight, 'fsdp', axis=0, tiled=True)  632 us
    all_gather x1, waiting for transfers between devices, body(): lax.all_gather(down_weight, 'fsdp', axis=0, tiled=True)  621 us
    reduce_scatter x1, waiting for transfers between devices, body(): lax.psum_scatter(matmul_tn(act_low, grad_mlp).astype(jnp.bfloat16), 'fsdp...  546 us
    reduce_scatter x1, waiting for transfers between devices, body(): lax.psum_scatter(matmul_tn(normed_two, grad_pre).astype(jnp.bfloat16), 'f...  546 us
    reduce_scatter x1, waiting for transfers between devices, body(): lax.psum_scatter(grad_output_weight.astype(jnp.bfloat16), 'fsdp', scatter...  153 us
    psum x1, waiting for transfers between devices, body(): lax.psum(shard_query_weight.astype(jnp.bfloat16), 'ctx').astype(jnp.float32)  112 us
    all_gather x1, waiting for transfers between devices, body(): lax.all_gather(output_weight, 'fsdp', axis=0, tiled=True)  111 us
    reduce_scatter x1, waiting for transfers between devices, body(): lax.psum_scatter(grad_query_weight.astype(jnp.bfloat16), 'fsdp', scatter_...  105 us
  transfers between devices with their start and end apart: 12, of which 10 were waited for; matrix products, arithmetic and copies ran while one was open for 3% of the time, Pallas kernels for 0%

commit v1 on v0

v1 whole, which is shorter than its diff:
```python
import functools
import math

import jax
import jax.numpy as jnp
from jax import lax
from jax.experimental import pallas as pl
from jax.experimental.pallas import tpu as pltpu
from jax.sharding import Mesh, PartitionSpec as P

H = 16
HD = 128
EPSILON = 1e-05
CLIP_LIMIT = 10.0
NEGATIVE = -1e30
BF = jnp.bfloat16
F32 = jnp.float32
GELU_A = 0.044715
GELU_C = math.sqrt(2.0 / math.pi)
SCALE = HD ** (-0.5)
MIB = 1 << 20


def mm(left, right):
    return jnp.dot(left, right, preferred_element_type=F32)


def mm_tn(left, right):
    return lax.dot_general(left, right, (((0,), (0,)), ((), ())), preferred_element_type=F32)


def mm_nt(left, right):
    return lax.dot_general(left, right, (((1,), (1,)), ((), ())), preferred_element_type=F32)


def shift(value, axis, count, step):
    return lax.ppermute(value, axis, [(i, (i + step) % count) for i in range(count)])


def pick(value, index, dim):
    return lax.dynamic_index_in_dim(value, index, dim, keepdims=False)


def in_order(parts, here, count, dim):
    if count == 1:
        return jnp.expand_dims(parts[0], dim)
    if count == 2:
        first = here == 0
        return jnp.stack(
            [jnp.where(first, parts[0], parts[1]), jnp.where(first, parts[1], parts[0])], dim
        )
    shape = list(parts[0].shape)
    shape.insert(dim, count)
    whole = jnp.zeros(shape, parts[0].dtype)
    for j, part in enumerate(parts):
        whole = lax.dynamic_update_index_in_dim(whole, part, lax.rem(here - j + count, count), dim)
    return whole


def gather(value, axis, count, dim):
    parts = [value] + [shift(value, axis, count, j) for j in range(1, count)]
    return in_order(parts, lax.axis_index(axis), count, dim)


def swap_blocks(value, axis, count, dim):
    here = lax.axis_index(axis)
    parts = [pick(value, here, dim)]
    for j in range(1, count):
        parts.append(shift(pick(value, lax.rem(here + j, count), dim), axis, count, j))
    return in_order(parts, here, count, dim)


def sum_blocks(value, axis, count, dim):
    here = lax.axis_index(axis)
    total = pick(value, here, dim).astype(F32)
    for j in range(1, count):
        block = pick(value, lax.rem(here + j, count), dim).astype(BF)
        total = total + shift(block, axis, count, j).astype(F32)
    return total


def sum_copies(value, axis, count):
    low = value.astype(BF)
    total = low.astype(F32)
    for j in range(1, count):
        total = total + shift(low, axis, count, j).astype(F32)
    return total


def attention_masks(rows, length):
    row = lax.broadcasted_iota(jnp.int32, (rows, rows), 0)
    col = lax.broadcasted_iota(jnp.int32, (rows, rows), 1)
    return (col <= row) & (col < length)


def attend_back_kernel(length_ref, q_ref, k_ref, v_ref, g_ref, gq_ref, gk_ref, gv_ref):
    rows = q_ref.shape[0]
    length = length_ref[0]
    scores = mm_nt(q_ref[...], k_ref[...]) * SCALE
    masked = jnp.where(attention_masks(rows, length), scores, NEGATIVE)
    top = jnp.max(masked, 1, keepdims=True)
    weights = jnp.exp(masked - top)
    weights = weights / jnp.sum(weights, 1, keepdims=True)
    grad_weights = mm_nt(g_ref[...], v_ref[...])
    delta = jnp.sum(weights * grad_weights, 1, keepdims=True)
    grad_scores = (weights * (grad_weights - delta)).astype(BF)
    gq_ref[...] = (mm(grad_scores, k_ref[...]) * SCALE).astype(BF)
    grad_keys = mm_tn(grad_scores, q_ref[...]) * SCALE
    grad_values = mm_tn(weights.astype(BF), g_ref[...])

    @pl.when(pl.program_id(0) == 0)
    def _():
        gk_ref[...] = grad_keys
        gv_ref[...] = grad_values

    @pl.when(pl.program_id(0) > 0)
    def _():
        gk_ref[...] += grad_keys
        gv_ref[...] += grad_values


def attend_back(length, queries, keys, values, grads):
    rows, width = queries.shape
    heads = width // HD
    block = pl.BlockSpec((rows, HD), lambda n, s: (0, n))
    whole = pl.BlockSpec((rows, HD), lambda n, s: (0, 0))
    return pl.pallas_call(
        attend_back_kernel,
        grid_spec=pltpu.PrefetchScalarGridSpec(
            num_scalar_prefetch=1,
            grid=(heads,),
            in_specs=[block, whole, whole, block],
            out_specs=[block, whole, whole],
        ),
        out_shape=[
            jax.ShapeDtypeStruct((rows, width), BF),
            jax.ShapeDtypeStruct((rows, HD), F32),
            jax.ShapeDtypeStruct((rows, HD), F32),
        ],
        compiler_params=pltpu.CompilerParams(vmem_limit_bytes=48 * MIB),
        cost_estimate=pl.CostEstimate(
            flops=10 * heads * rows * rows * HD,
            bytes_accessed=8 * rows * width,
            transcendentals=heads * rows * rows,
        ),
        name="attend_back",
    )(length, queries, keys, values, grads)


MESH = pl.DeviceIdType.MESH
SEMS = 96
SMALL_ROWS = 16


class Links:
    def __init__(self, sends, recvs, locals_):
        self.sends, self.recvs, self.locals_ = sends, recvs, locals_
        self.used, self.used_local = 0, 0
        self.open = []

    def push(self, src, dst, axis, target):
        index = self.used
        self.used += 1
        copy = pltpu.make_async_remote_copy(
            src_ref=src,
            dst_ref=dst,
            send_sem=self.sends.at[index],
            recv_sem=self.recvs.at[index],
            device_id={axis: target},
            device_id_type=MESH,
        )
        copy.start()
        self.open.append(copy)
        return copy

    def local(self, src, dst):
        index = self.used_local
        self.used_local += 1
        copy = pltpu.make_async_copy(src, dst, self.locals_.at[index])
        copy.start()
        return copy

    def drain(self):
        for copy in self.open:
            copy.wait_send()


def wait_all(copies):
    for copy in copies:
        copy.wait()


def wait_recvs(copies):
    for copy in copies:
        copy.wait_recv()


def around(axis, here, count):
    return [(axis, lax.rem(here + j, count)) for j in range(1, count)]


def greet(groups):
    barrier = pltpu.get_barrier_semaphore()
    count = 0
    for group in groups:
        for axis, target in group:
            pl.semaphore_signal(barrier, inc=1, device_id={axis: target}, device_id_type=MESH)
            count += 1
    pl.semaphore_wait(barrier, count)


class Gather:
    def __init__(self, links, buf, place):
        self.links, self.buf, (self.z, self.Z, self.x, self.X) = links, buf, place
        block = buf.at[self.z * self.X + self.x]
        self.from_z = [links.push(block, block, *to) for to in around("z", self.z, self.Z)]
        self.from_x = [links.push(block, block, *to) for to in around("x", self.x, self.X)]

    def forward(self, j):
        self.from_z[j - 1].wait_recv()
        block = self.buf.at[lax.rem(self.z - j + self.Z, self.Z) * self.X + self.x]
        self.from_x += [
            self.links.push(block, block, *to) for to in around("x", self.x, self.X)
        ]

    def finish(self):
        wait_recvs(self.from_x)


def forward_kernel(
    sizes,
    length_ref,
    rows,
    gmlp,
    wq,
    wkv,
    small,
    wo,
    up,
    down,
    seq_o,
    wqkv_o,
    wo_o,
    wup,
    wdown,
    gmall,
    ntall,
    normed_o,
    qkv_o,
    att_o,
    mid_o,
    top_o,
    vec_o,
    v_seq,
    v_hat,
    v_norm,
    v_w,
    v_small,
    v_vec,
    v_qkv,
    v_att,
    v_wo,
    v_br,
    v_brall,
    v_mid,
    v_nt,
    v_top,
    v_topz,
    v_topx,
    v_tall,
    sends,
    recvs,
    locals_,
):
    Y, K, Z, X = sizes
    C, S = Y * K, Z * X
    y, k, z, x = (lax.axis_index(name) for name in ("y", "k", "z", "x"))
    c = y * K + k
    me = z * X + x
    R, D = rows.shape
    T = C * R
    cols = D // C
    qkv_cols = cols + 2 * HD
    here = wq.shape[0]
    part = wdown.shape[1]
    heads = cols // HD
    length = length_ref[0]
    links = Links(sends, recvs, locals_)
    place = (z, Z, x, X)
    to_z, to_x = around("z", z, Z), around("x", x, X)
    to_y, to_k = around("y", y, Y), around("k", k, K)
    zs = [lax.rem(z - j + Z, Z) for j in range(Z)]
    ys = [lax.rem(y - j + Y, Y) for j in range(Y)]
    others = [
        (jy, jk, lax.rem(y + jy, Y), lax.rem(k + jk, K))
        for jy in range(Y)
        for jk in range(K)
        if jy or jk
    ]

    greet([to_z, to_x, to_y, to_k])

    first = [
        links.local(wq.at[:, pl.ds(pl.multiple_of(c * cols, cols), cols)], v_w.at[me, :, pl.ds(0, cols)]),
        links.local(wkv, v_w.at[me, :, pl.ds(cols, 2 * HD)]),
        links.local(small, v_small.at[me]),
        links.local(rows, v_seq.at[pl.ds(c * R, R)]),
    ]
    own_wo = links.local(wo.at[:, pl.ds(pl.multiple_of(c * cols, cols), cols)], v_wo.at[me])
    wait_all(first)
    qkv_gather = Gather(links, v_w, place)
    small_gather = Gather(links, v_small, place)
    mine = v_seq.at[pl.ds(c * R, R)]
    seq_y = [links.push(mine, mine, *to) for to in to_y]
    seq_k = [links.push(mine, mine, *to) for to in to_k]
    for j in range(1, Y):
        seq_y[j - 1].wait_recv()
        block = v_seq.at[pl.ds((ys[j] * K + k) * R, R)]
        seq_k += [links.push(block, block, *to) for to in to_k]
    wait_recvs(seq_k)
    save_seq = links.local(v_seq, seq_o)

    step = 64

    @pl.loop(0, T // step)
    def _(i):
        span = pl.ds(pl.multiple_of(i * step, step), step)
        values = v_seq[span, :].astype(F32)
        center = values - jnp.mean(values, 1, keepdims=True)
        rstd = lax.rsqrt(jnp.mean(center * center, 1, keepdims=True) + EPSILON)
        v_hat[span, :] = center * rstd

    for j in (1, Z - 1, 2):
        qkv_gather.forward(j)
        small_gather.forward(j)
    own_wo.wait()
    wo_gather = Gather(links, v_wo, place)
    qkv_gather.finish()
    small_gather.finish()

    own_up = []
    up_z = []
    up_x = []
    for j in range(Z):
        target = lax.rem(z + j, Z)
        for i in range(X):
            unit = ((target * X + i) * K + k) * part
            src = up.at[:, pl.ds(pl.multiple_of(unit, part), part)]
            dst = wup.at[me, :, pl.ds(i * part, part)]
            if j == 0:
                own_up.append(links.local(src, dst))
            else:
                up_z.append(links.push(src, dst, "z", target))
    own_down = links.local(down.at[pl.ds(pl.multiple_of(k * part, part), part)], wdown.at[x])
    down_x = [
        links.push(down.at[pl.ds(pl.multiple_of(k * part, part), part)], wdown.at[x], *to)
        for to in to_x
    ]
    own_gm = links.local(gmlp, gmall.at[z, k])
    gm_z = [links.push(gmlp, gmall.at[z, k], *to) for to in to_z]
    gm_k = [links.push(gmlp, gmall.at[z, k], *to) for to in to_k]

    for s in range(S):
        v_vec[:, pl.ds(s * here, here)] = v_small[s]
    gain = v_vec[0:1, :].astype(F32)
    bias = v_vec[1:2, :].astype(F32)

    @pl.loop(0, T // step)
    def _(i):
        span = pl.ds(pl.multiple_of(i * step, step), step)
        v_norm[span, :] = (v_hat[span, :] * gain + bias).astype(BF)

    save_norm = links.local(v_norm, normed_o)
    save_vec = links.local(v_vec, vec_o)
    q_bias = v_vec[2:3, pl.ds(pl.multiple_of(c * cols, cols), cols)].astype(F32)
    v_bias = jnp.zeros((1, HD), F32)
    for s in range(S):
        v_bias = v_bias + v_small[s, 12:13, 0:HD].astype(F32)
    wide = min(cols, 256)
    for n in range(cols // wide):
        span = slice(n * wide, (n + 1) * wide)
        weights = v_w[:, :, span].reshape(D, wide)
        v_qkv[:, span] = (mm(v_norm[...], weights) + q_bias[:, span]).astype(BF)
    weights = v_w[:, :, cols:].reshape(D, 2 * HD)
    kv_bias = jnp.concatenate([jnp.zeros((1, HD), F32), v_bias], 1)
    v_qkv[:, cols:] = (mm(v_norm[...], weights) + kv_bias).astype(BF)
    save_qkv = links.local(v_qkv, qkv_o)

    @pl.loop(0, heads)
    def _(n):
        span = pl.ds(pl.multiple_of(n * HD, HD), HD)
        scores = mm_nt(v_qkv[:, span], v_qkv[:, cols : cols + HD]) * SCALE
        masked = jnp.where(attention_masks(T, length), scores, NEGATIVE)
        top = jnp.max(masked, 1, keepdims=True)
        weights = jnp.exp(masked - top)
        probs = (weights / jnp.sum(weights, 1, keepdims=True)).astype(BF)
        own = pl.ds(pl.multiple_of(c * cols + n * HD, HD), HD)
        v_att[:, own] = mm(probs, v_qkv[:, cols + HD :]).astype(BF)
        live = lax.broadcasted_iota(jnp.int32, (T, 1), 0) < length
        best = jnp.max(jnp.where(live, top, NEGATIVE), 0, keepdims=True)
        v_top[pl.ds(n, 1), :] = jnp.broadcast_to(best, (1, HD))

    def att_block(source):
        return v_att.at[:, pl.ds(pl.multiple_of(source * cols, cols), cols)]

    att_y = [links.push(att_block(c), att_block(c), *to) for to in to_y]
    att_k = [links.push(att_block(c), att_block(c), *to) for to in to_k]
    top_z = [links.push(v_top, v_topz.at[j], *to) for j, to in enumerate(to_z)]
    for j in (1, Z - 1, 2):
        wo_gather.forward(j)
    for j in range(1, Y):
        att_y[j - 1].wait_recv()
        att_k += [links.push(att_block(ys[j] * K + k), att_block(ys[j] * K + k), *to) for to in to_k]
    wait_recvs(top_z)
    best = v_top[...]
    for j in range(Z - 1):
        best = jnp.maximum(best, v_topz[j])
    v_topx[0] = best
    top_x = [links.push(v_topx.at[0], v_topx.at[j + 1], *to) for j, to in enumerate(to_x)]
    wait_recvs(att_k)
    save_att = links.local(v_att, att_o)
    wo_gather.finish()

    narrow = min(cols, 256)
    for n in range(cols // narrow):
        span = slice(n * narrow, (n + 1) * narrow)
        weights = v_wo[:, :, span].reshape(D, narrow)
        v_br[:, :, span] = mm(v_att[...], weights).astype(BF).reshape(C, R, narrow)
    br_in = []
    for jy, jk, ty, tk in others:
        index = links.used
        links.used += 1
        copy = pltpu.make_async_remote_copy(
            src_ref=v_br.at[ty * K + tk],
            dst_ref=v_brall.at[c],
            send_sem=sends.at[index],
            recv_sem=recvs.at[index],
            device_id={"y": ty, "k": tk},
            device_id_type=MESH,
        )
        copy.start()
        links.open.append(copy)
        br_in.append(copy)
    v_brall[c] = v_br[c]
    wait_recvs(top_x)
    best = v_topx[0]
    for j in range(1, X):
        best = jnp.maximum(best, v_topx[j])
    v_tall[c] = best
    top_y = [links.push(v_tall.at[c], v_tall.at[c], *to) for to in to_y]
    top_k = [links.push(v_tall.at[c], v_tall.at[c], *to) for to in to_k]
    wait_recvs(br_in)

    for q in range(C):
        span = slice(q * cols, (q + 1) * cols)
        rows_in = v_seq[pl.ds(pl.multiple_of(c * R, R), R), span].astype(F32)
        v_mid[:, span] = rows_in + v_brall[q].astype(F32) + v_vec[3:4, span].astype(F32)
    save_mid = links.local(v_mid, mid_o)
    gain_two = v_vec[4:5, :].astype(F32)
    bias_two = v_vec[5:6, :].astype(F32)

    @pl.loop(0, R // step)
    def _(i):
        span = pl.ds(pl.multiple_of(i * step, step), step)
        values = v_mid[span, :]
        center = values - jnp.mean(values, 1, keepdims=True)
        rstd = lax.rsqrt(jnp.mean(center * center, 1, keepdims=True) + EPSILON)
        v_nt[span, :] = (center * rstd * gain_two + bias_two).astype(BF)

    own_nt = links.local(v_nt, ntall.at[z, k])
    nt_z = [links.push(v_nt, ntall.at[z, k], *to) for to in to_z]
    nt_k = [links.push(v_nt, ntall.at[z, k], *to) for to in to_k]

    for j in range(1, Y):
        top_y[j - 1].wait_recv()
        block = v_tall.at[ys[j] * K + k]
        top_k += [links.push(block, block, *to) for to in to_k]
    wait_recvs(top_k)
    save_top = links.local(v_tall, top_o)

    wait_all(own_up)
    up_x += [links.push(wup.at[me], wup.at[me], *to) for to in to_x]
    for j in (1, Z - 1, 2):
        wait_recvs(up_z[(j - 1) * X : j * X])
        block = wup.at[zs[j] * X + x]
        up_x += [links.push(block, block, *to) for to in to_x]
    for j in (1, Z - 1, 2):
        gm_z[j - 1].wait_recv()
        gm_k += [links.push(gmall.at[zs[j], k], gmall.at[zs[j], k], *to) for to in to_k]
    for j in (1, Z - 1, 2):
        nt_z[j - 1].wait_recv()
        nt_k += [links.push(ntall.at[zs[j], k], ntall.at[zs[j], k], *to) for to in to_k]
    save_w = links.local(v_w, wqkv_o)
    save_wo = links.local(v_wo, wo_o)
    wait_recvs(down_x + up_x + gm_k + nt_k)
    wait_all(
        [own_down, own_gm, own_nt, save_seq, save_norm, save_vec, save_qkv, save_att, save_mid]
        + [save_top, save_w, save_wo]
    )
    links.drain()


def forward_call(sizes, lengths, rows, gmlp, wq, wkv, small, wo, up, down):
    Y, K, Z, X = sizes
    C, S = Y * K, Z * X
    R, D = rows.shape
    T = C * R
    cols = D // C
    qkv_cols = cols + 2 * HD
    here = wq.shape[0]
    part = down.shape[0] // K
    heads = cols // HD
    shape = jax.ShapeDtypeStruct
    anywhere = pl.BlockSpec(memory_space=pl.ANY)
    outs = [
        shape((T, D), BF),
        shape((S, here, qkv_cols), BF),
        shape((S, here, cols), BF),
        shape((S, here, X * part), BF),
        shape((X, part, D), BF),
        shape((Z, K, R, D), BF),
        shape((Z, K, R, D), BF),
        shape((T, D), BF),
        shape((T, qkv_cols), BF),
        shape((T, D), BF),
        shape((R, D), F32),
        shape((C, 8, HD), F32),
        shape((SMALL_ROWS, D), BF),
    ]
    return pl.pallas_call(
        functools.partial(forward_kernel, sizes),
        in_specs=[pl.BlockSpec(memory_space=pltpu.SMEM)] + [anywhere] * 8,
        out_specs=[anywhere] * len(outs),
        out_shape=outs,
        scratch_shapes=[
            pltpu.VMEM((T, D), BF),
            pltpu.VMEM((T, D), F32),
            pltpu.VMEM((T, D), BF),
            pltpu.VMEM((S, here, qkv_cols), BF),
            pltpu.VMEM((S, SMALL_ROWS, here), BF),
            pltpu.VMEM((SMALL_ROWS, D), BF),
            pltpu.VMEM((T, qkv_cols), BF),
            pltpu.VMEM((T, D), BF),
            pltpu.VMEM((S, here, cols), BF),
            pltpu.VMEM((C, R, cols), BF),
            pltpu.VMEM((C, R, cols), BF),
            pltpu.VMEM((R, D), F32),
            pltpu.VMEM((R, D), BF),
            pltpu.VMEM((8, HD), F32),
            pltpu.VMEM((Z - 1, 8, HD), F32),
            pltpu.VMEM((X, 8, HD), F32),
            pltpu.VMEM((C, 8, HD), F32),
            pltpu.SemaphoreType.DMA((SEMS,)),
            pltpu.SemaphoreType.DMA((SEMS,)),
            pltpu.SemaphoreType.DMA((32,)),
        ],
        compiler_params=pltpu.CompilerParams(
            collective_id=1, has_side_effects=True, vmem_limit_bytes=60 * MIB
        ),
        name="layer_forward",
    )(lengths, rows, gmlp, wq, wkv, small, wo, up, down)


def norm_parts(values):
    center = values - jnp.mean(values, -1, keepdims=True)
    rstd = lax.rsqrt(jnp.mean(center * center, -1, keepdims=True) + EPSILON)
    return center * rstd, rstd


def norm_back(grad, gain, xhat, rstd):
    scaled = grad * gain
    return rstd * (
        scaled
        - jnp.mean(scaled, -1, keepdims=True)
        - xhat * jnp.mean(scaled * xhat, -1, keepdims=True)
    )


def body(
    sizes,
    inputs,
    lengths,
    norm1_gain,
    norm1_bias,
    query_weight,
    query_bias,
    keyval_weight,
    value_bias,
    output_weight,
    output_bias,
    norm2_gain,
    norm2_bias,
    up_weight,
    up_bias,
    down_weight,
    down_bias,
    cotangent,
):
    Y, K, Z, X = sizes
    C, S = Y * K, Z * X
    y, k, z, x = (lax.axis_index(name) for name in ("y", "k", "z", "x"))
    c = y * K + k
    R, D = inputs.shape[1:]
    rows_here = query_weight.shape[0]
    ff_here = down_weight.shape[0]
    ff_part = ff_here // K
    FF = ff_here * S
    T = C * R
    cols = D // C
    heads = H // C
    qkv_cols = cols + 2 * HD
    small_len = 7 * rows_here + ff_here + HD // S
    small_rows = -(-small_len // qkv_cols)
    small_rows = -(-small_rows // 16) * 16
    packed_rows = rows_here + small_rows

    pieces = [norm1_gain, norm1_bias, query_bias, output_bias, norm2_gain, norm2_bias, down_bias]
    shard = z * X + x
    lanes = jnp.arange(HD) // (HD // S) == shard
    value_row = jnp.where(lanes, jnp.tile(value_bias, S), 0).astype(BF)
    small = jnp.zeros((SMALL_ROWS, rows_here), BF)
    for row, piece in enumerate(pieces):
        small = small + jnp.pad(piece[None, :], ((row, SMALL_ROWS - 1 - row), (0, 0)))
    small = small + jnp.pad(up_bias.reshape(-1, rows_here), ((8, 4), (0, 0)))
    small = small + jnp.pad(value_row[None, :], ((12, 3), (0, rows_here - HD)))

    length = lengths[0]
    positions = c * R + jnp.arange(R, dtype=jnp.int32)
    live_rows = (positions < length).astype(F32)[:, None]
    grad_out = live_rows * cotangent[0].astype(F32)
    grad_mlp = grad_out.astype(BF)
    rows_low = inputs[0]
    (
        seq_low,
        wqkv,
        wo,
        wup,
        wdown,
        grad_mlp_all,
        normed_two_all,
        normed,
        qkv,
        attended_all,
        middle,
        tops,
        vectors,
    ) = forward_call(
        sizes,
        lengths,
        rows_low,
        grad_mlp,
        query_weight,
        keyval_weight,
        small,
        output_weight,
        up_weight,
        down_weight,
    )
    wqkv = wqkv.reshape(D, qkv_cols)
    wo = wo.reshape(D, cols)
    wup = wup.reshape(D, X * ff_part)
    wdown = wdown.reshape(X * ff_part, D)
    grad_mlp_all = grad_mlp_all.reshape(Z * K * R, D)
    normed_two_all = normed_two_all.reshape(Z * K * R, D)
    queries, keys, values = qkv[:, :cols], qkv[:, cols : cols + HD], qkv[:, cols + HD :]
    top_logit = tops[:, :heads, 0].reshape(H)
    gain_one = vectors[0].astype(F32)
    gain_two = vectors[4].astype(F32)
    d_bias = vectors[6].astype(F32)
    u_bias = vectors[8:12].reshape(K, 4 // K, Z, X, rows_here)
    u_bias_own = pick(pick(u_bias, k, 0), z, 1)
    u_bias_own = jnp.moveaxis(u_bias_own, 0, 1).reshape(-1).astype(F32)
    rows_in = rows_low.astype(F32)
    seq_hat, seq_rstd = norm_parts(seq_low.astype(F32))
    hat_two, rstd_two = norm_parts(middle)

    pre_act = mm(normed_two_all, wup) + u_bias_own
    tanh = jnp.tanh(GELU_C * (pre_act + GELU_A * pre_act * pre_act * pre_act))
    act = (0.5 * pre_act * (1.0 + tanh)).astype(BF)
    slope = 0.5 * (1.0 + tanh) + 0.5 * pre_act * (1.0 - tanh * tanh) * GELU_C * (
        1.0 + 3.0 * GELU_A * pre_act * pre_act
    )
    grad_act = mm_nt(grad_mlp_all, wdown)
    grad_pre_wide = grad_act * slope
    grad_pre = grad_pre_wide.astype(BF)
    grad_two_part = mm_nt(grad_pre, wup).astype(BF)
    grad_two = lax.psum_scatter(grad_two_part, ("z", "k"), tiled=True).astype(F32)
    mlp_part = mm(act, wdown).astype(BF)
    mlp_out = lax.psum_scatter(mlp_part, ("z", "k"), tiled=True).astype(F32)
    result = (live_rows * (middle + mlp_out + d_bias)).astype(BF)[None]

    grad_up_bias = jnp.sum(grad_pre.astype(F32), 0)
    grad_down_bias = jnp.sum(grad_mlp.astype(F32), 0)

    gdown = mm_tn(act, grad_mlp_all).astype(BF).reshape(X, ff_part, D)
    gdown = sum_blocks(gdown, "x", X, 0)
    gdown = sum_copies(gdown, "y", Y).astype(BF)
    grad_down_weight = gather(gdown, "k", K, 0).reshape(ff_here, D).astype(F32)

    gup = mm_tn(normed_two_all, grad_pre).astype(BF)
    gup = gup.reshape(Z, X, Y, rows_here // Y, X * ff_part)
    gup = sum_blocks(gup, "x", X, 1)
    gup = sum_blocks(gup, "y", Y, 1).astype(BF)
    gup = swap_blocks(gup, "z", Z, 0)
    gup = gather(gather(gup, "y", Y, 0), "k", K, 1)
    gup = gup.reshape(Y, K, Z, rows_here // Y, X, ff_part).transpose(0, 3, 2, 4, 1, 5)
    grad_up_weight = gup.reshape(rows_here, FF).astype(F32)

    grad_gain_two = jnp.sum(grad_two * hat_two, 0)
    grad_shift_two = jnp.sum(grad_two, 0)
    grad_middle = grad_out + norm_back(grad_two, gain_two, hat_two, rstd_two)
    grad_branch = grad_middle.astype(BF)
    grad_output_bias = jnp.sum(grad_branch.astype(F32), 0)
    grad_branch_cols = swap_blocks(grad_branch.reshape(R, C, cols), ("y", "k"), C, 1)
    grad_branch_cols = jnp.moveaxis(grad_branch_cols, 1, 0).reshape(T, cols)
    grad_att = mm_nt(grad_branch_cols, wo).astype(BF).reshape(T, Y, K, cols)
    grad_att = sum_blocks(grad_att, "k", K, 2)
    grad_att = sum_blocks(grad_att, "y", Y, 1).astype(BF)
    gout = mm_tn(attended_all, grad_branch_cols).astype(BF).reshape(Z, X, rows_here, cols)
    gout = sum_blocks(gout, "x", X, 1).astype(BF)
    gout = lax.psum_scatter(gout, "z")
    gout = gather(gather(gout, "y", Y, 1), "k", K, 2)
    grad_output_weight = gout.reshape(rows_here, D).astype(F32)

    grad_queries, grad_keys, grad_values = attend_back(lengths, queries, keys, values, grad_att)
    grad_qkv = jnp.concatenate([grad_queries, grad_keys.astype(BF), grad_values.astype(BF)], 1)
    grad_one_part = mm_nt(grad_qkv, wqkv)
    grad_gain_one = jnp.sum(grad_one_part * seq_hat, 0)
    grad_shift_one = jnp.sum(grad_one_part, 0)
    grad_one = grad_one_part.astype(BF).reshape(Y, K, R, D)
    grad_one = sum_blocks(grad_one, "k", K, 1)
    grad_one = sum_blocks(grad_one, "y", Y, 0)
    hat_one, rstd_one = norm_parts(rows_in)
    input_grad = (grad_middle + norm_back(grad_one, gain_one, hat_one, rstd_one)).astype(BF)[None]

    gqkv = mm_tn(normed, grad_qkv).astype(BF).reshape(Z, X, rows_here, qkv_cols)
    qkv_bias_grad = jnp.sum(grad_qkv.astype(F32), 0)
    grad_query_bias = lax.dynamic_update_slice_in_dim(
        jnp.zeros((D,), F32), qkv_bias_grad[:cols], c * cols, 0
    )
    grad_up_bias_all = lax.dynamic_update_slice(
        jnp.zeros((Z, X, K, ff_part), F32),
        grad_up_bias.reshape(1, X, 1, ff_part),
        (z, 0, k, 0),
    ).reshape(S, ff_here)
    small_grads = jnp.concatenate(
        [
            item.reshape(S, rows_here)
            for item in (
                grad_gain_one,
                grad_shift_one,
                grad_query_bias,
                grad_output_bias,
                grad_gain_two,
                grad_shift_two,
                grad_down_bias,
            )
        ]
        + [grad_up_bias_all, qkv_bias_grad[cols + HD :].reshape(S, HD // S)],
        1,
    )
    small_grads = jnp.pad(small_grads, ((0, 0), (0, small_rows * qkv_cols - small_len)))
    small_grads = small_grads.astype(BF).reshape(Z, X, small_rows, qkv_cols)
    gpacked = jnp.concatenate([gqkv, small_grads], 2)
    gpacked = sum_blocks(gpacked, "x", X, 1).astype(BF)
    gpacked = lax.psum_scatter(gpacked, "z")
    gpacked = gather(gather(gpacked, "y", Y, 0), "k", K, 1).reshape(C, packed_rows, qkv_cols)
    grad_query_weight = (
        jnp.moveaxis(gpacked[:, :rows_here, :cols], 0, 1).reshape(rows_here, D).astype(F32)
    )
    grad_keyval_weight = jnp.sum(gpacked[:, :rows_here, cols:].astype(F32), 0)
    small_sums = jnp.sum(gpacked[:, rows_here:].astype(F32), 0).reshape(-1)
    place = 0
    small_outs = []
    for size in [rows_here] * 7 + [ff_here, HD // S]:
        small_outs.append(small_sums[place : place + size])
        place += size

    factors = CLIP_LIMIT / jnp.maximum(top_logit, CLIP_LIMIT)
    column_scale = jnp.repeat(jnp.sqrt(factors), HD)
    clipped_query_weight = (query_weight.astype(F32) * column_scale[None, :]).astype(BF)
    bias_scale = lax.dynamic_slice_in_dim(column_scale, shard * rows_here, rows_here, 0)
    clipped_query_bias = (query_bias.astype(F32) * bias_scale).astype(BF)
    key_scale = jnp.sqrt(jnp.min(factors))
    keyval_scale = jnp.concatenate([jnp.ones((HD,), F32) * key_scale, jnp.ones((HD,), F32)])
    clipped_keyval_weight = (keyval_weight.astype(F32) * keyval_scale[None, :]).astype(BF)

    return (
        result,
        input_grad,
        small_outs[0],
        small_outs[1],
        grad_query_weight,
        small_outs[2],
        grad_keyval_weight,
        small_outs[8],
        grad_output_weight,
        small_outs[3],
        small_outs[4],
        small_outs[5],
        grad_up_weight,
        small_outs[7],
        grad_down_weight,
        small_outs[6],
        clipped_query_weight,
        clipped_query_bias,
        clipped_keyval_weight,
    )


def solution(mesh):
    ctx, fsdp = mesh.shape["ctx"], mesh.shape["fsdp"]
    sizes = (ctx // 2, 2, 4, fsdp // 4)
    fine = Mesh(mesh.devices.reshape(sizes), ("y", "k", "z", "x"))
    tokens = P(("z", "x"), ("y", "k"), None)
    vector = P(("z", "x"))
    matrix = P(("z", "x"), None)
    return jax.shard_map(
        functools.partial(body, sizes),
        mesh=fine,
        in_specs=(
            tokens, vector, vector, vector, matrix, vector, matrix, vector, matrix, vector,
            vector, vector, matrix, vector, matrix, vector, tokens,
        ),
        out_specs=(
            tokens, tokens, vector, vector, matrix, vector, matrix, vector, matrix, vector,
            vector, vector, matrix, vector, matrix, vector, matrix, vector, matrix,
        ),
        check_vma=False,
    )
```

time: 3360 us -> 642 us (0.19)
  waiting for transfers between devices: 2870 us -> 170 us
  blocking collectives: 263 us -> 0 us
  Pallas kernels: 0 us -> 220 us
  matrix products: 148 us -> 55.8 us
  local copies, waits for them, and re-layouts: 10.5 us -> 83.4 us
  other arithmetic: 33 us -> 68.7 us
    all_gather x5 -> x0, waiting for transfers between devices: 1370 us -> none  [the longest x1 632 us: body(): lax.all_gather(up_weight, 'fsdp', axis=0, tiled=True)]
    reduce_scatter x5 -> x4, waiting for transfers between devices: 1350 us -> 0.02 us  [the longest x1 0.02 us: body(): gpacked = lax.psum_scatter(gpacked, 'z')]
    pallas_call x0 -> x2, Pallas kernels: none -> 220 us  [the longest x1 214 us: forward_call(): pl.pallas_call(functools.partial(forward_kernel, sizes), in_specs=[pl.Blo...]
    ppermute x0 -> x23, waiting for transfers between devices: none -> 170 us  [shift(): lax.ppermute(value, axis, [(i, (i + step) % count) for i in range(count)])]
    all_gather x9 -> x0, blocking collectives: 161 us -> none  [the longest x1 26.3 us: body(): lax.all_gather(up_bias, 'fsdp', axis=0, tiled=True)]
    psum x1 -> x0, waiting for transfers between devices: 112 us -> none  [body(): lax.psum(shard_query_weight.astype(jnp.bfloat16), 'ctx').astype(jnp.float32)]
    dot_general x24 -> x10, matrix products: 148 us -> 55.8 us  [the longest x4 18.9 us: mm_tn(): lax.dot_general(left, right, (((0,), (0,)), ((), ())), preferred_element_...]
    unnamed x2 -> x0, blocking collectives: 53.5 us -> none
  transfers between devices with their start and end apart: 12 -> 27, of which waited for: 10 -> 10; matrix products, arithmetic and copies ran while one was open for 3% -> 26% of each run, Pallas kernels for 0% -> 1%
where the time goes in v1:
time: 642 us; the launch traced here: 631 us
  Pallas kernels  220 us (34%)
  waiting for transfers between devices  170 us (26%)
  local copies, waits for them, and re-layouts  83.4 us (13%)
  other arithmetic  68.7 us (11%)
  matrix products  55.8 us (9%)
  between operations  16.6 us (3%)
  starting transfers between devices  16.1 us (3%)
    pallas_call x1, Pallas kernels, forward_call(): pl.pallas_call(functools.partial(forward_kernel, sizes), in_specs=[pl.Blo...  214 us
    ppermute x23, waiting for transfers between devices, shift(): lax.ppermute(value, axis, [(i, (i + step) % count) for i in range(count)])  170 us
    convert_element_type x2, local copies, waits for them, and re-layouts, body(): grad_up_weight = gup.reshape(rows_here, FF).astype(F32)  25.1 us
    dot_general x4, matrix products, mm_tn(): lax.dot_general(left, right, (((0,), (0,)), ((), ())), preferred_element_...  18.9 us
    dot_general x4, matrix products, mm_nt(): lax.dot_general(left, right, (((1,), (1,)), ((), ())), preferred_element_...  18.9 us
    dot_general x2, matrix products, mm(): return jnp.dot(left, right, preferred_element_type=F32)  18 us
    ppermute x23, starting transfers between devices, shift(): lax.ppermute(value, axis, [(i, (i + step) % count) for i in range(count)])  15.2 us
  transfers between devices with their start and end apart: 27, of which 10 were waited for; matrix products, arithmetic and copies ran while one was open for 26% of the time, Pallas kernels for 1%

profile of v1, /device:TPU:0, one launch (start us, length us, event | category | flops | bytes accessed | tf_op | source)
XLA Modules:
  0.0 631.0 jit_solution(17325624474724345166)
XLA Ops:
  16.6 214.2 %layer_forward.1 = (bf16[512,2048]{1,0:T(8,128)(2,1)}, bf16[8,256,768]{2,1,0:T(8,128)(2,1)}, bf16[8,256,512]{2,1,0:T(8,128)(2,1)}, bf16[8,256,1024]{2,1,0:T(8,12...) custom-call(s32[1]{0:T(128)} %copy.124.length_ref, ...), custom_call_target="tpu_custom_call" | custom-call | tf_op jit(solution)/shard_map/layer_forward/pallas_call | solution.py:530
  231.7 7.7 %fusion.56 = f32[1024,1024]{1,0:T(8,128)S(1)} fusion(bf16[1024,2048]{1,0:T(8,128)(2,1)} %bitcast.243, bf16[2048,1024]{1,0:T(8,128)(2,1)} %bitcast.247), kind=kOutput, calls=%fused_computation.185 | convolution fusion | flops 4294967296 | bytes 12582912 | tf_op jit(solution)/shard_map/dot_general | solution.py:25
  239.4 7.0 %convert_reduce_fusion.1 = (f32[1024]{0:T(1024)S(1)}, bf16[1024,1024]{1,0:T(8,128)(2,1)S(1)}) fusion(f32[1024,1024]{1,0:T(8,128)S(1)} %fusion.56, f32[1024]{0:T(1024)S(1)} %bitcast.238, bf16[1024,2048]{1,0:T(8,128)(2,1)S(1)} %bitcast.241, bf16[1024,2048]{1,0:T(8,128)(2,1)S(1)} %bitcast.246), kind=kOutput, calls=%fused_computation.25 | convolution fusion | flops 4318034944 | bytes 14688256 | tf_op jit(solution)/shard_map/dot_general | solution.py:33
  246.5 6.1 convolution_convert_fusion.2
  253.1 10.4 %convolution_convert_fusion.3 = bf16[1024,2048]{1,0:T(8,128)(2,1)} fusion(bf16[1024,2048]{1,0:T(8,128)(2,1)} %bitcast.245, f32[1024,1024]{1,0:T(8,128)} %copy-done.33, f32[1024]{0:T(1024)S(1)} %bitcast.239), kind=kOutput, calls=%fused_computation.30 | convolution fusion | flops 4307550208 | bytes 12587008 | tf_op jit(solution)/shard_map/dot_general | solution.py:25
  263.6 7.1 %convolution_convert_fusion.1 = bf16[2048,1024]{1,0:T(8,128)(2,1)S(1)} fusion(bf16[1024,2048]{1,0:T(8,128)(2,1)} %bitcast.244, bf16[1024,1024]{1,0:T(8,128)(2,1)S(1)} %get-tuple-element.127), kind=kOutput, calls=%fused_computation.28 | convolution fusion | flops 4297064448 | bytes 10485760 | tf_op jit(solution)/shard_map/dot_general | solution.py:29
  275.9 5.3 convolution_convert_fusion
  290.7 32.2 %collective-permute-done.13 = bf16[4,2,128,1024]{3,2,0,1:T(8,128)(2,1)} collective-permute-done((bf16[4,2,128,1024]{3,2,0,1:T(8,128)(2,1)}, bf16[4,2,128,1024]{3,2,0,1:T(8,128)(2,1)}, u32[]{:S(2)}, u32[]{:S(2)}) %collective-permute-start.13) | collective-permute-done | bytes 2097184 | tf_op jit(solution)/shard_map/ppermute | solution.py:37
  322.9 3.3 convert_add_fusion.1
  330.0 36.2 %collective-permute-done.20 = bf16[512,2048]{1,0:T(8,128)(2,1)} collective-permute-done((bf16[512,2048]{1,0:T(8,128)(2,1)}, bf16[512,2048]{1,0:T(8,128)(2,1)}, u32[]{:S(2)}, u32[]{:S(2)}) %collective-permute-start.20) | collective-permute-done | bytes 2097184 | tf_op jit(solution)/shard_map/ppermute | solution.py:37
  366.2 4.5 fusion.12
  384.8 32.3 %collective-permute-done = bf16[128,512]{1,0:T(8,128)(2,1)S(1)} collective-permute-done((bf16[128,512]{1,0:T(8,128)(2,1)S(1)}, bf16[128,512]{1,0:T(8,128)(2,1)S(1)}, u32[]{:S(2)}, u32[]{:S(2)}) %collective-permute-start) | collective-permute-done | bytes 131104 | tf_op jit(solution)/shard_map/ppermute | solution.py:37
  417.7 4.4 collective-permute-done.1
  428.1 2.9 copy.62
  442.6 3.0 convolution_convert_fusion.5
  450.5 3.0 add_convert_fusion
  453.7 18.1 %collective-permute-done.10 = bf16[4,256,512]{2,1,0:T(8,128)(2,1)} collective-permute-done((bf16[4,256,512]{2,1,0:T(8,128)(2,1)}, bf16[4,256,512]{2,1,0:T(8,128)(2,1)}, u32[]{:S(2)}, u32[]{:S(2)}) %collective-permute-start.10) | collective-permute-done | bytes 1048608 | tf_op jit(solution)/shard_map/ppermute | solution.py:37
  478.8 5.7 attend_back.1
  484.7 3.5 convolution_convert_fusion.4
  488.2 3.1 fusion.48
  504.0 28.4 %collective-permute-done.7 = bf16[4,272,768]{2,1,0:T(8,128)(2,1)} collective-permute-done((bf16[4,272,768]{2,1,0:T(8,128)(2,1)}, bf16[4,272,768]{2,1,0:T(8,128)(2,1)}, u32[]{:S(2)}, u32[]{:S(2)}) %collective-permute-start.7) | collective-permute-done | bytes 1671200 | tf_op jit(solution)/shard_map/ppermute | solution.py:37
  532.4 3.1 fusion.13
  538.3 4.7 bitcast_convert_fusion
  545.8 4.1 broadcast_select_fusion.1
  549.9 4.2 copy.74
  554.1 3.9 copy.73
  558.1 6.2 convert_bitcast_fusion
  564.2 13.3 %copy.75 = f32[2,128,4,2,2,512]{5,4,3,2,1,0:T(2,128)} copy(f32[2,128,4,2,2,512]{1,5,3,2,0,4:T(8,128)} %convert_bitcast_fusion) | data formatting | bytes 16777216 | tf_op jit(solution)/shard_map/convert_element_type | solution.py:707
  577.6 11.8 %reshape.343 = f32[256,8192]{1,0:T(8,128)} reshape(f32[2,128,4,2,2,512]{5,4,3,2,1,0:T(2,128)} %copy.75) | data formatting | bytes 16777216 | tf_op jit(solution)/shard_map/convert_element_type | solution.py:707
  591.9 6.8 %collective-permute-done.11 = bf16[256,512]{1,0:T(8,128)(2,1)S(1)} collective-permute-done((bf16[256,512]{1,0:T(8,128)(2,1)}, bf16[256,512]{1,0:T(8,128)(2,1)S(1)}, u32[]{:S(2)}, u32[]{:S(2)}) %collective-permute-start.11) | collective-permute-done | bytes 262176 | tf_op jit(solution)/shard_map/ppermute | solution.py:37
  599.8 7.2 %collective-permute-done.8 = bf16[272,768]{1,0:T(8,128)(2,1)S(1)} collective-permute-done((bf16[272,768]{1,0:T(8,128)(2,1)}, bf16[272,768]{1,0:T(8,128)(2,1)S(1)}, u32[]{:S(2)}, u32[]{:S(2)}) %collective-permute-start.8) | collective-permute-done | bytes 417824 | tf_op jit(solution)/shard_map/ppermute | solution.py:37
  621.1 2.9 copy.76
  (254 shorter events, 107.8 us)
Async XLA Ops:
  7.2 370.6 %reduce-scatter.7.cloned.1.call-start = ((), (), s32[]{:S(2)}) async-start(), calls=%async_computation.5 | async-start | bytes 4718592 | tf_op jit(solution)/shard_map/reduce_scatter | solution.py:687
  252.6 125.2 %reduce-scatter.5.cloned.1.call-start = ((), (), s32[]{:S(2)}) async-start(), calls=%async_computation.4 | async-start | bytes 4718592 | tf_op jit(solution)/shard_map/reduce_scatter | solution.py:689
  263.5 325.8 %reduce-scatter.11.cloned.1.call-start = ((), (), s32[]{:S(2)}) async-start(), calls=%async_computation.7 | async-start | bytes 1310720 | tf_op jit(solution)/shard_map/reduce_scatter | solution.py:721
  274.0 48.9 %collective-permute-start.13 = (bf16[4,2,128,1024]{3,2,0,1:T(8,128)(2,1)}, bf16[4,2,128,1024]{3,2,0,1:T(8,128)(2,1)}, u32[]{:S(2)}, u32[]{:S(2)}) collective-permute-start(bf16[4,2,128,1024]{3,2,0,1:T(8,128)(2,1)} %bitcast.198), channel_id=1, source_target_pairs={{0,1},{1,0},{2,3},{3,2},{4,5},{5,4},{6,7},{7,6},{8,9},{9,8},{10,11... | collective-permute-start | bytes 6291464 | tf_op jit(solution)/shard_map/ppermute | solution.py:37
  284.8 81.4 %collective-permute-start.20 = (bf16[512,2048]{1,0:T(8,128)(2,1)}, bf16[512,2048]{1,0:T(8,128)(2,1)}, u32[]{:S(2)}, u32[]{:S(2)}) collective-permute-start(bf16[512,2048]{1,0:T(8,128)(2,1)} %dynamic-slice_bitcast_fusion), channel_id=1, source_target_pairs={{0,1},{1,0},{2,3},{3,2},{4,5},{5,4},{6,7},{7,6},{8,9},{9,8},{10,11... | collective-permute-start | bytes 6291464 | tf_op jit(solution)/shard_map/ppermute | solution.py:37
  327.4 43.8 %collective-permute-start.14 = (bf16[4,128,1024]{2,1,0:T(8,128)(2,1)}, bf16[4,128,1024]{2,1,0:T(8,128)(2,1)S(1)}, u32[]{:S(2)}, u32[]{:S(2)}) collective-permute-start(bf16[4,128,1024]{2,1,0:T(8,128)(2,1)} %fusion.38), channel_id=1, source_target_pairs={{0,16},{16,0},{1,17},{17,1},{2,18},{18,2},{3,19},{19,3},{4,20},{20... | collective-permute-start | bytes 3145736 | tf_op jit(solution)/shard_map/ppermute | solution.py:37
  329.0 42.2 %copy-start.3 = (f32[4,2,128,1024]{3,2,0,1:T(8,128)S(1)}, f32[4,2,128,1024]{3,2,0,1:T(8,128)}, u32[]{:S(2)}) copy-start(f32[4,2,128,1024]{3,2,0,1:T(8,128)} %copy-done.2) | copy-start | bytes 12582916
  370.7 79.9 %collective-permute-start.21 = (bf16[512,2048]{1,0:T(8,128)(2,1)}, bf16[512,2048]{1,0:T(8,128)(2,1)}, u32[]{:S(2)}, u32[]{:S(2)}) collective-permute-start(bf16[512,2048]{1,0:T(8,128)(2,1)} %fusion.12), channel_id=1, source_target_pairs={{0,16},{16,0},{1,17},{17,1},{2,18},{18,2},{3,19},{19,3},{4,20},{20... | collective-permute-start | bytes 6291464 | tf_op jit(solution)/shard_map/ppermute | solution.py:37
  373.6 61.9 %collective-permute-start.15 = (bf16[128,1024]{1,0:T(8,128)(2,1)}, bf16[128,1024]{1,0:T(8,128)(2,1)}, u32[]{:S(2)}, u32[]{:S(2)}) collective-permute-start(bf16[128,1024]{1,0:T(8,128)(2,1)} %get-tuple-element.99), channel_id=1, source_target_pairs={{0,2},{2,4},{4,6},{6,0},{1,3},{3,5},{5,7},{7,1},{8,10},{10,12},{12... | collective-permute-start | bytes 786440 | tf_op jit(solution)/shard_map/ppermute | solution.py:37
  375.3 61.9 %collective-permute-start.16 = (bf16[128,1024]{1,0:T(8,128)(2,1)}, bf16[128,1024]{1,0:T(8,128)(2,1)}, u32[]{:S(2)}, u32[]{:S(2)}) collective-permute-start(bf16[128,1024]{1,0:T(8,128)(2,1)} %get-tuple-element.98), channel_id=1, source_target_pairs={{0,4},{2,6},{4,0},{6,2},{1,5},{3,7},{5,1},{7,3},{8,12},{10,14},{12... | collective-permute-start | bytes 786440 | tf_op jit(solution)/shard_map/ppermute | solution.py:37
  377.4 61.5 %collective-permute-start.17 = (bf16[128,1024]{1,0:T(8,128)(2,1)}, bf16[128,1024]{1,0:T(8,128)(2,1)}, u32[]{:S(2)}, u32[]{:S(2)}) collective-permute-start(bf16[128,1024]{1,0:T(8,128)(2,1)} %get-tuple-element.97), channel_id=1, source_target_pairs={{0,6},{2,0},{4,2},{6,4},{1,7},{3,1},{5,3},{7,5},{8,14},{10,8},{12,... | collective-permute-start | bytes 786440 | tf_op jit(solution)/shard_map/ppermute | solution.py:37
  383.5 42.0 %copy-start.32 = (bf16[8,256,512]{2,1,0:T(8,128)(2,1)S(1)}, bf16[8,256,512]{2,1,0:T(8,128)(2,1)}, u32[]{:S(2)}) copy-start(bf16[8,256,512]{2,1,0:T(8,128)(2,1)} %get-tuple-element.42) | copy-start | bytes 6291460
  384.6 32.5 %collective-permute-start = (bf16[128,512]{1,0:T(8,128)(2,1)S(1)}, bf16[128,512]{1,0:T(8,128)(2,1)S(1)}, u32[]{:S(2)}, u32[]{:S(2)}) collective-permute-start(bf16[128,512]{1,0:T(8,128)(2,1)S(1)} %bitcast.229), channel_id=1, source_target_pairs={{0,8},{8,16},{16,24},{24,0},{1,9},{9,17},{17,25},{25,1},{2,10},{10... | collective-permute-start | bytes 393224 | tf_op jit(solution)/shard_map/ppermute | solution.py:37
  417.1 5.0 collective-permute-start.1
  422.1 2.5 collective-permute-start.2
  434.8 12.6 %collective-permute-start.3 = (bf16[512,2,512]{2,0,1:T(8,128)(2,1)}, bf16[512,2,512]{2,0,1:T(8,128)(2,1)}, u32[]{:S(2)}, u32[]{:S(2)}) collective-permute-start(bf16[512,2,512]{2,0,1:T(8,128)(2,1)} %bitcast.23), channel_id=1, source_target_pairs={{0,8},{8,0},{1,9},{9,1},{2,10},{10,2},{3,11},{11,3},{4,12},{12,4},... | collective-permute-start | bytes 3145736 | tf_op jit(solution)/shard_map/ppermute | solution.py:37
  440.6 59.1 %collective-permute-start.18 = (bf16[4,128,1024]{2,1,0:T(8,128)(2,1)}, bf16[4,128,1024]{2,1,0:T(8,128)(2,1)}, u32[]{:S(2)}, u32[]{:S(2)}) collective-permute-start(bf16[4,128,1024]{2,1,0:T(8,128)(2,1)} %bitcast_dynamic-update-slice_fusion), channel_id=1, source_target_pairs={{0,16},{16,0},{1,17},{17,1},{2,18},{18,2},{3,19},{19,3},{4,20},{20... | collective-permute-start | bytes 3145736 | tf_op jit(solution)/shard_map/ppermute | solution.py:37
  446.7 25.1 %collective-permute-start.10 = (bf16[4,256,512]{2,1,0:T(8,128)(2,1)}, bf16[4,256,512]{2,1,0:T(8,128)(2,1)}, u32[]{:S(2)}, u32[]{:S(2)}) collective-permute-start(bf16[4,256,512]{2,1,0:T(8,128)(2,1)} %dynamic-slice_bitcast_fusion.1), channel_id=1, source_target_pairs={{0,1},{1,0},{2,3},{3,2},{4,5},{5,4},{6,7},{7,6},{8,9},{9,8},{10,11... | collective-permute-start | bytes 3145736 | tf_op jit(solution)/shard_map/ppermute | solution.py:37
  449.9 27.4 %collective-permute-start.4 = (bf16[512,512]{1,0:T(8,128)(2,1)}, bf16[512,512]{1,0:T(8,128)(2,1)}, u32[]{:S(2)}, u32[]{:S(2)}) collective-permute-start(bf16[512,512]{1,0:T(8,128)(2,1)} %fusion.43), channel_id=1, source_target_pairs={{0,16},{16,0},{1,17},{17,1},{2,18},{18,2},{3,19},{19,3},{4,20},{20... | collective-permute-start | bytes 1572872 | tf_op jit(solution)/shard_map/ppermute | solution.py:37
  453.5 82.0 %collective-permute-start.22 = (bf16[512,2048]{1,0:T(8,128)(2,1)S(1)}, bf16[512,2048]{1,0:T(8,128)(2,1)}, u32[]{:S(2)}, u32[]{:S(2)}) collective-permute-start(bf16[512,2048]{1,0:T(8,128)(2,1)S(1)} %add_convert_fusion), channel_id=1, source_target_pairs={{0,8},{8,0},{1,9},{9,1},{2,10},{10,2},{3,11},{11,3},{4,12},{12,4},... | collective-permute-start | bytes 6291464 | tf_op jit(solution)/shard_map/ppermute | solution.py:37
  474.7 115.7 %reduce-scatter.9.cloned.1.call-start = ((), (), s32[]{:S(2)}) async-start(), calls=%async_computation.6 | async-start | bytes 2088960 | tf_op jit(solution)/shard_map/reduce_scatter | solution.py:766
  494.5 37.9 %collective-permute-start.7 = (bf16[4,272,768]{2,1,0:T(8,128)(2,1)}, bf16[4,272,768]{2,1,0:T(8,128)(2,1)}, u32[]{:S(2)}, u32[]{:S(2)}) collective-permute-start(bf16[4,272,768]{2,1,0:T(8,128)(2,1)} %fusion.17), channel_id=1, source_target_pairs={{0,1},{1,0},{2,3},{3,2},{4,5},{5,4},{6,7},{7,6},{8,9},{9,8},{10,11... | collective-permute-start | bytes 5013512 | tf_op jit(solution)/shard_map/ppermute | solution.py:37
  499.7 32.7 %copy-start.4 = (bf16[2048,768]{1,0:T(8,128)(2,1)S(1)}, bf16[2048,768]{1,0:T(8,128)(2,1)}, u32[]{:S(2)}) copy-start(bf16[2048,768]{1,0:T(8,128)(2,1)} %convolution_convert_fusion.4) | copy-start | bytes 9437188
  504.0 41.7 %collective-permute-start.19 = (bf16[2,4,128,1024]{3,2,1,0:T(8,128)(2,1)}, bf16[2,4,128,1024]{3,2,1,0:T(8,128)(2,1)}, u32[]{:S(2)}, u32[]{:S(2)}) collective-permute-start(bf16[2,4,128,1024]{3,2,1,0:T(8,128)(2,1)} %pad_maximum_fusion.1), channel_id=1, source_target_pairs={{0,8},{8,0},{1,9},{9,1},{2,10},{10,2},{3,11},{11,3},{4,12},{12,4},... | collective-permute-start | bytes 6291464 | tf_op jit(solution)/shard_map/ppermute | solution.py:37
  537.8 5.2 collective-permute-start.5
  544.3 45.6 %collective-permute-start.6 = (bf16[128,2048]{1,0:T(8,128)(2,1)}, bf16[128,2048]{1,0:T(8,128)(2,1)S(1)}, u32[]{:S(2)}, u32[]{:S(2)}) collective-permute-start(bf16[128,2048]{1,0:T(8,128)(2,1)} %fusion.44), channel_id=1, source_target_pairs={{0,16},{16,0},{1,17},{17,1},{2,18},{18,2},{3,19},{19,3},{4,20},{20... | collective-permute-start | bytes 1572872 | tf_op jit(solution)/shard_map/ppermute | solution.py:37
  589.3 9.3 %collective-permute-start.11 = (bf16[256,512]{1,0:T(8,128)(2,1)}, bf16[256,512]{1,0:T(8,128)(2,1)S(1)}, u32[]{:S(2)}, u32[]{:S(2)}) collective-permute-start(bf16[256,512]{1,0:T(8,128)(2,1)} %bitcast.226), channel_id=1, source_target_pairs={{0,16},{16,0},{1,17},{17,1},{2,18},{18,2},{3,19},{19,3},{4,20},{20... | collective-permute-start | bytes 786440 | tf_op jit(solution)/shard_map/ppermute | solution.py:37
  589.9 9.9 %copy-start.19 = (bf16[128,2048]{1,0:T(8,128)(2,1)}, bf16[128,2048]{1,0:T(8,128)(2,1)S(1)}, u32[]{:S(2)}) copy-start(bf16[128,2048]{1,0:T(8,128)(2,1)S(1)} %collective-permute-done.6) | copy-start | bytes 1572868
  590.4 18.7 %copy-start.12 = (f32[128,2048]{1,0:T(8,128)S(1)}, f32[128,2048]{1,0:T(8,128)}, u32[]{:S(2)}) copy-start(f32[128,2048]{1,0:T(8,128)} %get-tuple-element.83) | copy-start | bytes 3145732
  590.4 16.6 %collective-permute-start.8 = (bf16[272,768]{1,0:T(8,128)(2,1)}, bf16[272,768]{1,0:T(8,128)(2,1)S(1)}, u32[]{:S(2)}, u32[]{:S(2)}) collective-permute-start(bf16[272,768]{1,0:T(8,128)(2,1)} %bitcast.225), channel_id=1, source_target_pairs={{0,16},{16,0},{1,17},{17,1},{2,18},{18,2},{3,19},{19,3},{4,20},{20... | collective-permute-start | bytes 1253384 | tf_op jit(solution)/shard_map/ppermute | solution.py:37
  599.7 10.7 %collective-permute-start.12 = (bf16[256,2,512]{2,0,1:T(8,128)(2,1)S(1)}, bf16[256,2,512]{2,0,1:T(8,128)(2,1)S(1)}, u32[]{:S(2)}, u32[]{:S(2)}) collective-permute-start(bf16[256,2,512]{2,0,1:T(8,128)(2,1)S(1)} %pad_maximum_fusion.5), channel_id=1, source_target_pairs={{0,8},{8,0},{1,9},{9,1},{2,10},{10,2},{3,11},{11,3},{4,12},{12,4},... | collective-permute-start | bytes 1572872 | tf_op jit(solution)/shard_map/ppermute | solution.py:37
  609.1 6.0 collective-permute-start.9
  (30 other events, 121.7 us)
Sparse Core Ops, SparseCore 0:
  252.7 48.9 reduce-scatter.6
  304.0 48.1 reduce-scatter.4
  474.8 29.0 reduce-scatter.10
  535.6 39.5 reduce-scatter.8

commit v2 on v1

--- a/solution.py
+++ b/solution.py
@@ -93,63 +93,36 @@
     return (col <= row) & (col < length)
 
 
-def attend_back_kernel(length_ref, q_ref, k_ref, v_ref, g_ref, gq_ref, gk_ref, gv_ref):
-    rows = q_ref.shape[0]
-    length = length_ref[0]
-    scores = mm_nt(q_ref[...], k_ref[...]) * SCALE
-    masked = jnp.where(attention_masks(rows, length), scores, NEGATIVE)
-    top = jnp.max(masked, 1, keepdims=True)
-    weights = jnp.exp(masked - top)
-    weights = weights / jnp.sum(weights, 1, keepdims=True)
-    grad_weights = mm_nt(g_ref[...], v_ref[...])
-    delta = jnp.sum(weights * grad_weights, 1, keepdims=True)
-    grad_scores = (weights * (grad_weights - delta)).astype(BF)
-    gq_ref[...] = (mm(grad_scores, k_ref[...]) * SCALE).astype(BF)
-    grad_keys = mm_tn(grad_scores, q_ref[...]) * SCALE
-    grad_values = mm_tn(weights.astype(BF), g_ref[...])
-
-    @pl.when(pl.program_id(0) == 0)
-    def _():
-        gk_ref[...] = grad_keys
-        gv_ref[...] = grad_values
-
-    @pl.when(pl.program_id(0) > 0)
-    def _():
-        gk_ref[...] += grad_keys
-        gv_ref[...] += grad_values
-
-
-def attend_back(length, queries, keys, values, grads):
-    rows, width = queries.shape
-    heads = width // HD
-    block = pl.BlockSpec((rows, HD), lambda n, s: (0, n))
-    whole = pl.BlockSpec((rows, HD), lambda n, s: (0, 0))
-    return pl.pallas_call(
-        attend_back_kernel,
-        grid_spec=pltpu.PrefetchScalarGridSpec(
-            num_scalar_prefetch=1,
-            grid=(heads,),
-            in_specs=[block, whole, whole, block],
-            out_specs=[block, whole, whole],
-        ),
-        out_shape=[
-            jax.ShapeDtypeStruct((rows, width), BF),
-            jax.ShapeDtypeStruct((rows, HD), F32),
-            jax.ShapeDtypeStruct((rows, HD), F32),
-        ],
-        compiler_params=pltpu.CompilerParams(vmem_limit_bytes=48 * MIB),
-        cost_estimate=pl.CostEstimate(
-            flops=10 * heads * rows * rows * HD,
-            bytes_accessed=8 * rows * width,
-            transcendentals=heads * rows * rows,
-        ),
-        name="attend_back",
-    )(length, queries, keys, values, grads)
-
-
 MESH = pl.DeviceIdType.MESH
-SEMS = 96
 SMALL_ROWS = 16
+
+
+def sem_count(sizes):
+    return 112 if sizes[0] * sizes[3] <= 4 else 240
+
+
+class Move:
+    def __init__(self, copy, send_if, recv_if):
+        self.copy, self.send_if, self.recv_if = copy, send_if, recv_if
+
+    def start(self):
+        guarded(self.send_if, self.copy.start)
+
+    def wait_send(self):
+        guarded(self.send_if, self.copy.wait_send)
+
+    def wait_recv(self):
+        guarded(self.recv_if, self.copy.wait_recv)
+
+
+def guarded(condition, action):
+    if condition is None:
+        action()
+    else:
+
+        @pl.when(condition)
+        def _():
+            action()
 
 
 class Links:
@@ -158,31 +131,87 @@
         self.used, self.used_local = 0, 0
         self.open = []
 
-    def push(self, src, dst, axis, target):
+    def plan(self, src, dst, where, send_if=None, recv_if=None):
         index = self.used
         self.used += 1
+        assert self.used <= self.sends.shape[0]
         copy = pltpu.make_async_remote_copy(
             src_ref=src,
             dst_ref=dst,
             send_sem=self.sends.at[index],
             recv_sem=self.recvs.at[index],
-            device_id={axis: target},
+            device_id=where,
             device_id_type=MESH,
         )
-        copy.start()
-        self.open.append(copy)
-        return copy
+        move = Move(copy, send_if, recv_if)
+        self.open.append(move)
+        return move
+
+    def push(self, src, dst, axis, target=None, when=None):
+        where = axis if isinstance(axis, dict) else {axis: target}
+        move = self.plan(src, dst, where, when, when)
+        move.start()
+        return move
+
+    def sent(self, moves):
+        for move in moves:
+            move.wait_send()
+            self.open = [other for other in self.open if other is not move]
 
     def local(self, src, dst):
         index = self.used_local
         self.used_local += 1
+        assert self.used_local < self.locals_.shape[0]
         copy = pltpu.make_async_copy(src, dst, self.locals_.at[index])
         copy.start()
         return copy
 
     def drain(self):
-        for copy in self.open:
-            copy.wait_send()
+        for move in self.open:
+            move.wait_send()
+
+
+class Line:
+    def __init__(self, links, block, z, Z, source=None):
+        self.z, self.Z = z, Z
+        self.hops = []
+        right, left = {"z": jnp.minimum(z + 1, Z - 1)}, {"z": jnp.maximum(z - 1, 0)}
+        for h in range(1, Z):
+            low, high = jnp.maximum(z - h + 1, 0), jnp.minimum(z + h - 1, Z - 1)
+            ahead, back = block(low), block(high)
+            own = source is not None and h == 1
+            self.hops.append(
+                [
+                    links.plan(
+                        source if own else ahead,
+                        ahead,
+                        right,
+                        (z >= h - 1) & (z < Z - 1),
+                        z >= h,
+                    ),
+                    links.plan(
+                        source if own else back,
+                        back,
+                        left,
+                        (z <= Z - h) & (z > 0),
+                        z < Z - h,
+                    ),
+                ]
+            )
+        for move in self.hops[0]:
+            move.start()
+
+    def hop(self, h):
+        for move in self.hops[h - 1]:
+            move.wait_recv()
+        if h < self.Z - 1:
+            for move in self.hops[h]:
+                move.start()
+        z, Z = self.z, self.Z
+        return [
+            (jnp.maximum(z - h, 0), z >= h),
+            (jnp.minimum(z + h, Z - 1), z < Z - h),
+        ]
 
 
 def wait_all(copies):
@@ -199,29 +228,31 @@
     return [(axis, lax.rem(here + j, count)) for j in range(1, count)]
 
 
-def greet(groups):
+def greet(groups, corners):
     barrier = pltpu.get_barrier_semaphore()
     count = 0
-    for group in groups:
-        for axis, target in group:
-            pl.semaphore_signal(barrier, inc=1, device_id={axis: target}, device_id_type=MESH)
-            count += 1
+    for where in [{axis: target} for group in groups for axis, target in group] + corners:
+        pl.semaphore_signal(barrier, inc=1, device_id=where, device_id_type=MESH)
+        count += 1
     pl.semaphore_wait(barrier, count)
 
 
 class Gather:
     def __init__(self, links, buf, place):
         self.links, self.buf, (self.z, self.Z, self.x, self.X) = links, buf, place
-        block = buf.at[self.z * self.X + self.x]
-        self.from_z = [links.push(block, block, *to) for to in around("z", self.z, self.Z)]
-        self.from_x = [links.push(block, block, *to) for to in around("x", self.x, self.X)]
-
-    def forward(self, j):
-        self.from_z[j - 1].wait_recv()
-        block = self.buf.at[lax.rem(self.z - j + self.Z, self.Z) * self.X + self.x]
+        self.line = Line(links, lambda at: buf.at[at * self.X + self.x], self.z, self.Z)
+        self.from_x = []
+        self.spread(self.z, None)
+
+    def spread(self, at, when):
+        block = self.buf.at[at * self.X + self.x]
         self.from_x += [
-            self.links.push(block, block, *to) for to in around("x", self.x, self.X)
+            self.links.push(block, block, *to, when=when) for to in around("x", self.x, self.X)
         ]
+
+    def hop(self, h):
+        for at, when in self.line.hop(h):
+            self.spread(at, when)
 
     def finish(self):
         wait_recvs(self.from_x)
@@ -292,13 +323,18 @@
     zs = [lax.rem(z - j + Z, Z) for j in range(Z)]
     ys = [lax.rem(y - j + Y, Y) for j in range(Y)]
     others = [
-        (jy, jk, lax.rem(y + jy, Y), lax.rem(k + jk, K))
+        (lax.rem(y + jy, Y), lax.rem(k + jk, K))
         for jy in range(Y)
         for jk in range(K)
         if jy or jk
     ]
-
-    greet([to_z, to_x, to_y, to_k])
+    corners = [
+        {"y": lax.rem(y + jy, Y), "k": lax.rem(k + jk, K)}
+        for jy in range(1, Y)
+        for jk in range(1, K)
+    ]
+
+    greet([to_z, to_x, to_y, to_k], corners)
 
     first = [
         links.local(wq.at[:, pl.ds(pl.multiple_of(c * cols, cols), cols)], v_w.at[me, :, pl.ds(0, cols)]),
@@ -317,6 +353,8 @@
         seq_y[j - 1].wait_recv()
         block = v_seq.at[pl.ds((ys[j] * K + k) * R, R)]
         seq_k += [links.push(block, block, *to) for to in to_k]
+    qkv_gather.hop(1)
+    small_gather.hop(1)
     wait_recvs(seq_k)
     save_seq = links.local(v_seq, seq_o)
 
@@ -330,35 +368,50 @@
         rstd = lax.rsqrt(jnp.mean(center * center, 1, keepdims=True) + EPSILON)
         v_hat[span, :] = center * rstd
 
-    for j in (1, Z - 1, 2):
-        qkv_gather.forward(j)
-        small_gather.forward(j)
+    qkv_gather.hop(2)
+    small_gather.hop(2)
     own_wo.wait()
     wo_gather = Gather(links, v_wo, place)
-    qkv_gather.finish()
-    small_gather.finish()
-
-    own_up = []
-    up_z = []
-    up_x = []
+    qkv_gather.hop(3)
+    small_gather.hop(3)
+
+    slab = here // Y
+    slab_y = pl.ds(pl.multiple_of(y * slab, slab), slab)
+    own_up, up_z, up_x, up_y = [], [], [], []
     for j in range(Z):
         target = lax.rem(z + j, Z)
         for i in range(X):
-            unit = ((target * X + i) * K + k) * part
-            src = up.at[:, pl.ds(pl.multiple_of(unit, part), part)]
-            dst = wup.at[me, :, pl.ds(i * part, part)]
+            unit = pl.ds(pl.multiple_of(((target * X + i) * K + k) * part, part), part)
+            side = pl.ds(i * part, part)
             if j == 0:
-                own_up.append(links.local(src, dst))
+                own_up.append(links.local(up.at[:, unit], wup.at[me, :, side]))
             else:
-                up_z.append(links.push(src, dst, "z", target))
+                up_z.append(
+                    links.push(up.at[slab_y, unit], wup.at[me, slab_y, side], "z", target)
+                )
+
+    def up_on(at, axis, to):
+        block = wup.at[at, slab_y]
+        return links.push(block, block, *to)
+
+    qkv_gather.finish()
+    small_gather.finish()
+    piece = part // Y
     own_down = links.local(down.at[pl.ds(pl.multiple_of(k * part, part), part)], wdown.at[x])
-    down_x = [
-        links.push(down.at[pl.ds(pl.multiple_of(k * part, part), part)], wdown.at[x], *to)
-        for to in to_x
-    ]
+    down_src = down.at[pl.ds(pl.multiple_of(k * part + y * piece, piece), piece)]
+    piece_y = pl.ds(pl.multiple_of(y * piece, piece), piece)
+    down_x = [links.push(down_src, wdown.at[x, piece_y], *to) for to in to_x]
     own_gm = links.local(gmlp, gmall.at[z, k])
-    gm_z = [links.push(gmlp, gmall.at[z, k], *to) for to in to_z]
+    gm_line = Line(links, lambda at: gmall.at[at, k], z, Z, gmlp)
     gm_k = [links.push(gmlp, gmall.at[z, k], *to) for to in to_k]
+
+    def gm_hop(h):
+        for at, when in gm_line.hop(h):
+            gm_k.extend(
+                links.push(gmall.at[at, k], gmall.at[at, k], *to, when=when) for to in to_k
+            )
+
+    wo_gather.hop(1)
 
     for s in range(S):
         v_vec[:, pl.ds(s * here, here)] = v_small[s]
@@ -385,6 +438,7 @@
     kv_bias = jnp.concatenate([jnp.zeros((1, HD), F32), v_bias], 1)
     v_qkv[:, cols:] = (mm(v_norm[...], weights) + kv_bias).astype(BF)
     save_qkv = links.local(v_qkv, qkv_o)
+    wo_gather.hop(2)
 
     @pl.loop(0, heads)
     def _(n):
@@ -406,8 +460,10 @@
     att_y = [links.push(att_block(c), att_block(c), *to) for to in to_y]
     att_k = [links.push(att_block(c), att_block(c), *to) for to in to_k]
     top_z = [links.push(v_top, v_topz.at[j], *to) for j, to in enumerate(to_z)]
-    for j in (1, Z - 1, 2):
-        wo_gather.forward(j)
+    wo_gather.hop(3)
+    gm_hop(1)
+    wait_all(own_up)
+    up_x += [up_on(me, "x", to) for to in to_x]
     for j in range(1, Y):
         att_y[j - 1].wait_recv()
         att_k += [links.push(att_block(ys[j] * K + k), att_block(ys[j] * K + k), *to) for to in to_k]
@@ -427,21 +483,19 @@
         weights = v_wo[:, :, span].reshape(D, narrow)
         v_br[:, :, span] = mm(v_att[...], weights).astype(BF).reshape(C, R, narrow)
     br_in = []
-    for jy, jk, ty, tk in others:
-        index = links.used
-        links.used += 1
-        copy = pltpu.make_async_remote_copy(
-            src_ref=v_br.at[ty * K + tk],
-            dst_ref=v_brall.at[c],
-            send_sem=sends.at[index],
-            recv_sem=recvs.at[index],
-            device_id={"y": ty, "k": tk},
-            device_id_type=MESH,
-        )
-        copy.start()
-        links.open.append(copy)
-        br_in.append(copy)
+    for ty, tk in others:
+        br_in.append(links.push(v_br.at[ty * K + tk], v_brall.at[c], {"y": ty, "k": tk}, None))
     v_brall[c] = v_br[c]
+    down_y = []
+    for j, move in enumerate(down_x):
+        move.wait_recv()
+        block = wdown.at[lax.rem(x - j - 1 + X, X), piece_y]
+        down_y += [links.push(block, block, *to) for to in to_y]
+    for j in (1, Z - 1, 2):
+        wait_recvs(up_z[(j - 1) * X : j * X])
+        up_x += [up_on(zs[j] * X + x, "x", to) for to in to_x]
+        up_y += [up_on(zs[j] * X + x, "y", to) for to in to_y]
+    gm_hop(2)
     wait_recvs(top_x)
     best = v_topx[0]
     for j in range(1, X):
@@ -468,8 +522,14 @@
         v_nt[span, :] = (center * rstd * gain_two + bias_two).astype(BF)
 
     own_nt = links.local(v_nt, ntall.at[z, k])
-    nt_z = [links.push(v_nt, ntall.at[z, k], *to) for to in to_z]
+    nt_line = Line(links, lambda at: ntall.at[at, k], z, Z, v_nt)
     nt_k = [links.push(v_nt, ntall.at[z, k], *to) for to in to_k]
+
+    def nt_hop(h):
+        for at, when in nt_line.hop(h):
+            nt_k.extend(
+                links.push(ntall.at[at, k], ntall.at[at, k], *to, when=when) for to in to_k
+            )
 
     for j in range(1, Y):
         top_y[j - 1].wait_recv()
@@ -478,21 +538,19 @@
     wait_recvs(top_k)
     save_top = links.local(v_tall, top_o)
 
-    wait_all(own_up)
-    up_x += [links.push(wup.at[me], wup.at[me], *to) for to in to_x]
-    for j in (1, Z - 1, 2):
-        wait_recvs(up_z[(j - 1) * X : j * X])
-        block = wup.at[zs[j] * X + x]
-        up_x += [links.push(block, block, *to) for to in to_x]
-    for j in (1, Z - 1, 2):
-        gm_z[j - 1].wait_recv()
-        gm_k += [links.push(gmall.at[zs[j], k], gmall.at[zs[j], k], *to) for to in to_k]
-    for j in (1, Z - 1, 2):
-        nt_z[j - 1].wait_recv()
-        nt_k += [links.push(ntall.at[zs[j], k], ntall.at[zs[j], k], *to) for to in to_k]
+    nt_hop(1)
+    order = [0, 1, Z - 1, 2]
+    for place_x, j in enumerate(order):
+        for i in range(1, X):
+            up_x[place_x * (X - 1) + i - 1].wait_recv()
+            block_at = zs[j] * X + lax.rem(x - i + X, X)
+            up_y += [up_on(block_at, "y", to) for to in to_y]
+    gm_hop(3)
+    nt_hop(2)
+    nt_hop(3)
     save_w = links.local(v_w, wqkv_o)
     save_wo = links.local(v_wo, wo_o)
-    wait_recvs(down_x + up_x + gm_k + nt_k)
+    wait_recvs(down_y + up_y + gm_k + nt_k)
     wait_all(
         [own_down, own_gm, own_nt, save_seq, save_norm, save_vec, save_qkv, save_att, save_mid]
         + [save_top, save_w, save_wo]
@@ -550,8 +608,8 @@
             pltpu.VMEM((Z - 1, 8, HD), F32),
             pltpu.VMEM((X, 8, HD), F32),
             pltpu.VMEM((C, 8, HD), F32),
-            pltpu.SemaphoreType.DMA((SEMS,)),
-            pltpu.SemaphoreType.DMA((SEMS,)),
+            pltpu.SemaphoreType.DMA((sem_count(sizes),)),
+            pltpu.SemaphoreType.DMA((sem_count(sizes),)),
             pltpu.SemaphoreType.DMA((32,)),
         ],
         compiler_params=pltpu.CompilerParams(
@@ -559,6 +617,625 @@
         ),
         name="layer_forward",
     )(lengths, rows, gmlp, wq, wkv, small, wo, up, down)
+
+
+def rows_loop(total, step, work):
+    @pl.loop(0, total // step)
+    def _(i):
+        work(pl.ds(pl.multiple_of(i * step, step), step))
+
+
+def backward_kernel(
+    sizes,
+    length_ref,
+    rows,
+    gmlp,
+    mid,
+    seq,
+    normed,
+    qkv,
+    att,
+    wqkv,
+    wo,
+    vec,
+    gub,
+    g2part,
+    mlppart,
+    gdown,
+    gup,
+    result_o,
+    igrad_o,
+    gdown_o,
+    gup_o,
+    gwo_o,
+    gwq_o,
+    gkv_o,
+    small_o,
+    h_dx,
+    h_dy,
+    h_ux,
+    h_us,
+    h_uy,
+    h_ds,
+    v_own,
+    v_kin,
+    v_zin,
+    m_own,
+    m_kin,
+    m_zin,
+    v_rows,
+    v_gm,
+    v_mid,
+    v_hat,
+    v_vec,
+    v_gbr,
+    v_gbc,
+    v_wo,
+    v_ga,
+    v_gak,
+    v_gay,
+    v_gatt,
+    v_big,
+    v_norm,
+    v_qkv,
+    v_gqkv,
+    v_gk,
+    v_gv,
+    v_wqkv,
+    v_dwo,
+    v_dwox,
+    v_dwoz,
+    v_dwq,
+    v_dwqx,
+    v_dwqz,
+    v_g1k,
+    v_g1y,
+    v_mean,
+    v_rstd,
+    v_sg,
+    v_sgb,
+    v_sgx,
+    v_sgz,
+    v_sga,
+    v_gub,
+    v_a,
+    v_b,
+    v_out,
+    sends,
+    recvs,
+    locals_,
+):
+    Y, K, Z, X = sizes
+    C, S = Y * K, Z * X
+    y, k, z, x = (lax.axis_index(name) for name in ("y", "k", "z", "x"))
+    c = y * K + k
+    me = z * X + x
+    R, D = rows.shape
+    T = C * R
+    cols = D // C
+    here = wqkv.shape[1]
+    part = gdown.shape[1]
+    heads = cols // HD
+    step = 64
+    length = length_ref[0]
+    links = Links(sends, recvs, locals_)
+    to_z, to_x = around("z", z, Z), around("x", x, X)
+    to_y, to_k = around("y", y, Y), around("k", k, K)
+    zs = [lax.rem(z - j + Z, Z) for j in range(Z)]
+    ys = [lax.rem(y - j + Y, Y) for j in range(Y)]
+    others = [
+        (lax.rem(y + jy, Y), lax.rem(k + jk, K))
+        for jy in range(Y)
+        for jk in range(K)
+        if jy or jk
+    ]
+    corners = [
+        {"y": lax.rem(y + jy, Y), "k": lax.rem(k + jk, K)}
+        for jy in range(1, Y)
+        for jk in range(1, K)
+    ]
+
+    greet([to_z, to_x, to_y, to_k], corners)
+
+    g2_k = [links.push(g2part.at[:, t], v_kin.at[j], a, t) for j, (a, t) in enumerate(to_k)]
+    own_g2 = links.local(g2part.at[:, k], v_own)
+    load = [
+        links.local(rows, v_rows),
+        links.local(gmlp, v_gm),
+        links.local(mid, v_mid),
+        links.local(vec, v_vec),
+        links.local(wo, v_wo),
+        links.local(gub, v_gub),
+        links.local(att, v_big),
+        links.local(qkv, v_qkv),
+        links.local(normed, v_norm),
+        links.local(wqkv, v_wqkv),
+    ]
+    gd_x = [links.push(gdown.at[t], h_dx.at[j], a, t) for j, (a, t) in enumerate(to_x)]
+    gu_x = [links.push(gup.at[:, t], h_ux.at[j], a, t) for j, (a, t) in enumerate(to_x)]
+
+    def add_into(own, extra, count):
+        for block in range(Z):
+
+            def work(span, block=block):
+                total = own[block, span, :].astype(F32)
+                for j in range(count):
+                    total = total + extra[j, block, span, :].astype(F32)
+                own[block, span, :] = total.astype(BF)
+
+            rows_loop(R, step, work)
+
+    own_g2.wait()
+    wait_recvs(g2_k)
+    add_into(v_own, v_kin, K - 1)
+    g2_z = [links.push(v_own.at[t], v_zin.at[j], a, t) for j, (a, t) in enumerate(to_z)]
+    mlp_k = [links.push(mlppart.at[:, t], m_kin.at[j], a, t) for j, (a, t) in enumerate(to_k)]
+    own_mlp = links.local(mlppart.at[:, k], m_own)
+    wait_all(load)
+
+    v_sg[...] = jnp.zeros_like(v_sg)
+
+    def second_norm(span):
+        values = v_mid[span, :]
+        center = values - jnp.mean(values, 1, keepdims=True)
+        rstd = lax.rsqrt(jnp.mean(center * center, 1, keepdims=True) + EPSILON)
+        v_hat[span, :] = center * rstd
+        v_rstd[span, :] = jnp.broadcast_to(rstd, (step, HD))
+        v_sg[6:7, :] += jnp.sum(v_gm[span, :].astype(F32), 0, keepdims=True)
+
+    rows_loop(R, step, second_norm)
+    own_mlp.wait()
+    wait_recvs(mlp_k)
+    add_into(m_own, m_kin, K - 1)
+    gain_two = v_vec[4:5, :].astype(F32)
+    wait_recvs(g2_z)
+
+    def second_back(span):
+        grad = v_own[z, span, :].astype(F32)
+        for j in range(Z - 1):
+            grad = grad + v_zin[j, span, :].astype(F32)
+        hat = v_hat[span, :]
+        v_sg[4:5, :] += jnp.sum(grad * hat, 0, keepdims=True)
+        v_sg[5:6, :] += jnp.sum(grad, 0, keepdims=True)
+        scaled = grad * gain_two
+        back = v_rstd[span, 0:1] * (
+            scaled
+            - jnp.mean(scaled, 1, keepdims=True)
+            - hat * jnp.mean(scaled * hat, 1, keepdims=True)
+        )
+        grad_middle = v_gm[span, :].astype(F32) + back
+        v_hat[span, :] = grad_middle
+        low = grad_middle.astype(BF)
+        v_sg[3:4, :] += jnp.sum(low.astype(F32), 0, keepdims=True)
+        for q in range(C):
+            v_gbr[q, span, :] = low[:, q * cols : (q + 1) * cols]
+
+    rows_loop(R, step, second_back)
+    gb = []
+    for ty, tk in others:
+        gb.append(links.push(v_gbr.at[ty * K + tk], v_gbc.at[c], {"y": ty, "k": tk}, None))
+    v_gbc[c] = v_gbr[c]
+    mlp_z = [links.push(m_own.at[t], m_zin.at[j], a, t) for j, (a, t) in enumerate(to_z)]
+    wait_recvs(gb)
+
+    grads_c = v_gbc[...].reshape(T, cols)
+    per = cols // here
+    for s in range(S):
+        span = slice((s % per) * here, (s % per + 1) * here)
+        v_ga[s // per, :, span] = mm_nt(grads_c, v_wo[s]).astype(BF)
+    ga_k = [
+        links.push(v_ga.at[q * K + t], v_gak.at[j, q], a, t)
+        for j, (a, t) in enumerate(to_k)
+        for q in range(Y)
+    ]
+    for s in range(S):
+        v_dwo[s // X, s % X] = mm_tn(
+            v_big[:, s * here : (s + 1) * here], v_gbc[...].reshape(T, cols)
+        ).astype(BF)
+    do_x = [links.push(v_dwo.at[:, t], v_dwox.at[j], a, t) for j, (a, t) in enumerate(to_x)]
+    load_seq = links.local(seq, v_big)
+    wait_recvs(ga_k)
+    for q in range(Y):
+
+        def ga_sum(span, q=q):
+            total = v_ga[q * K + k, span, :].astype(F32)
+            for j in range(K - 1):
+                total = total + v_gak[j, q, span, :].astype(F32)
+            v_gak[0, q, span, :] = total.astype(BF)
+
+        rows_loop(T, step, ga_sum)
+    ga_y = [links.push(v_gak.at[0, t], v_gay.at[j], a, t) for j, (a, t) in enumerate(to_y)]
+    load_seq.wait()
+
+    def stats(span):
+        values = v_big[span, :].astype(F32)
+        mean = jnp.mean(values, 1, keepdims=True)
+        center = values - mean
+        rstd = lax.rsqrt(jnp.mean(center * center, 1, keepdims=True) + EPSILON)
+        v_mean[span, :] = jnp.broadcast_to(mean, (step, HD))
+        v_rstd[span, :] = jnp.broadcast_to(rstd, (step, HD))
+
+    rows_loop(T, step, stats)
+    wait_recvs(ga_y)
+
+    def ga_last(span):
+        total = v_gak[0, y, span, :].astype(F32)
+        for j in range(Y - 1):
+            total = total + v_gay[j, span, :].astype(F32)
+        v_gatt[span, :] = total.astype(BF)
+
+    rows_loop(T, step, ga_last)
+
+    v_gk[...] = jnp.zeros_like(v_gk)
+    v_gv[...] = jnp.zeros_like(v_gv)
+
+    @pl.loop(0, heads)
+    def _(n):
+        span = pl.ds(pl.multiple_of(n * HD, HD), HD)
+        keys = v_qkv[:, cols : cols + HD]
+        scores = mm_nt(v_qkv[:, span], keys) * SCALE
+        masked = jnp.where(attention_masks(T, length), scores, NEGATIVE)
+        weights = jnp.exp(masked - jnp.max(masked, 1, keepdims=True))
+        weights = weights / jnp.sum(weights, 1, keepdims=True)
+        grads = v_gatt[:, span]
+        grad_weights = mm_nt(grads, v_qkv[:, cols + HD :])
+        delta = jnp.sum(weights * grad_weights, 1, keepdims=True)
+        grad_scores = (weights * (grad_weights - delta)).astype(BF)
+        v_gqkv[:, span] = (mm(grad_scores, keys) * SCALE).astype(BF)
+        v_gk[...] += mm_tn(grad_scores, v_qkv[:, span]) * SCALE
+        v_gv[...] += mm_tn(weights.astype(BF), grads)
+
+    v_gqkv[:, cols : cols + HD] = v_gk[...].astype(BF)
+    v_gqkv[:, cols + HD :] = v_gv[...].astype(BF)
+    for s in range(S):
+        v_dwq[s // X, s % X] = mm_tn(v_norm[:, s * here : (s + 1) * here], v_gqkv[...]).astype(BF)
+    dq_x = [links.push(v_dwq.at[:, t], v_dwqx.at[j], a, t) for j, (a, t) in enumerate(to_x)]
+
+    for s in range(S):
+        span = slice(s * here, (s + 1) * here)
+        grad = mm_nt(v_gqkv[...], v_wqkv[s])
+        v_norm[:, span] = grad.astype(BF)
+        hat = (v_big[:, span].astype(F32) - v_mean[:, 0:1]) * v_rstd[:, 0:1]
+        v_sg[0:1, span] = jnp.sum(grad * hat, 0, keepdims=True)
+        v_sg[1:2, span] = jnp.sum(grad, 0, keepdims=True)
+
+    def chunk(ref, q, t):
+        return ref.at[pl.ds(pl.multiple_of((q * K + t) * R, R), R)]
+
+    g1_k = [
+        links.push(chunk(v_norm, q, t), v_g1k.at[j, q], a, t)
+        for j, (a, t) in enumerate(to_k)
+        for q in range(Y)
+    ]
+
+    v_sg[2:3, pl.ds(pl.multiple_of(c * cols, cols), cols)] = jnp.sum(
+        v_gqkv[:, 0:cols].astype(F32), 0, keepdims=True
+    )
+    value_sum = jnp.sum(v_gqkv[:, cols + HD :].astype(F32), 0, keepdims=True)
+    for s in range(S):
+        v_sg[12:13, s * here : s * here + HD] = value_sum
+    units = part // here
+    for i in range(X):
+        to = pl.ds(pl.multiple_of((z * X + i) * here, here), here)
+        for r in range(units):
+            start = i * part + r * here
+            bias_part = v_gub[0:1, start : start + here]
+            for kk in range(K):
+                row = 8 + kk * units + r
+                v_sg[row : row + 1, to] = jnp.where(k == kk, bias_part, 0.0)
+    for s in range(S):
+        v_sgb[s // X, s % X] = v_sg[:, s * here : (s + 1) * here]
+    sg_x = [links.push(v_sgb.at[:, t], v_sgx.at[j], a, t) for j, (a, t) in enumerate(to_x)]
+
+    wait_recvs(gd_x)
+    half = v_a.shape[0]
+
+    def add_blocks(pairs, target, width):
+        count = target.shape[0]
+
+        @pl.loop(0, count // half)
+        def _(i):
+            span = pl.ds(pl.multiple_of(i * half, half), half)
+            sem = locals_.at[63]
+            for n, source in enumerate(pairs):
+                buf = v_a if n == 0 else v_b
+                copy = pltpu.make_async_copy(source.at[span], buf.at[:, pl.ds(0, width)], sem)
+                copy.start()
+                copy.wait()
+                if n > 0:
+
+                    def work(inner):
+                        v_out[inner, 0:width] = (
+                            (v_a if n == 1 else v_out)[inner, 0:width].astype(F32)
+                            + v_b[inner, 0:width].astype(F32)
+                        ).astype(BF)
+
+                    rows_loop(half, step, work)
+            copy = pltpu.make_async_copy(v_out.at[:, pl.ds(0, width)], target.at[span], sem)
+            copy.start()
+            copy.wait()
+
+    add_blocks([gdown.at[x]] + [h_dx.at[j] for j in range(X - 1)], gdown_o.at[k], D)
+    gd_y = [links.push(gdown_o.at[k], h_dy.at[j], *to) for j, to in enumerate(to_y)]
+
+    wait_recvs(gu_x)
+    for q in range(Z):
+        add_blocks(
+            [gup.at[q, x]] + [h_ux.at[j, q] for j in range(X - 1)], h_us.at[q], X * part
+        )
+    slab = here // Y
+
+    def slab_of(ref, t):
+        return ref.at[:, pl.ds(pl.multiple_of(t * slab, slab), slab)]
+
+    gu_y = [
+        links.push(slab_of(h_us, t), h_uy.at[j], a, t) for j, (a, t) in enumerate(to_y)
+    ]
+
+    wait_recvs(g1_k)
+    for q in range(Y):
+
+        def g1_sum(span, q=q):
+            own = pl.ds(pl.multiple_of((q * K + k) * R + span.start, step), step)
+            total = v_norm[own, :].astype(F32)
+            for j in range(K - 1):
+                total = total + v_g1k[j, q, span, :].astype(F32)
+            v_g1k[0, q, span, :] = total.astype(BF)
+
+        rows_loop(R, step, g1_sum)
+    g1_y = [links.push(v_g1k.at[0, t], v_g1y.at[j], a, t) for j, (a, t) in enumerate(to_y)]
+
+    def sum_x(own, extra, copies):
+        wait_recvs(copies)
+        for q in range(Z):
+            total = own[q, x].astype(F32)
+            for j in range(X - 1):
+                total = total + extra[j, q].astype(F32)
+            extra[0, q] = total.astype(extra.dtype)
+
+    sum_x(v_dwo, v_dwox, do_x)
+    do_z = [links.push(v_dwox.at[0, t], v_dwoz.at[j], a, t) for j, (a, t) in enumerate(to_z)]
+    sum_x(v_dwq, v_dwqx, dq_x)
+    dq_z = [links.push(v_dwqx.at[0, t], v_dwqz.at[j], a, t) for j, (a, t) in enumerate(to_z)]
+    sum_x(v_sgb, v_sgx, sg_x)
+    sg_z = [links.push(v_sgx.at[0, t], v_sgz.at[j], a, t) for j, (a, t) in enumerate(to_z)]
+
+    wait_recvs(gu_y)
+    for q in range(Z):
+        load_a = links.local(
+            h_us.at[q, pl.ds(pl.multiple_of(y * slab, slab), slab)],
+            v_a.at[pl.ds(0, slab), pl.ds(0, X * part)],
+        )
+        load_a.wait()
+        total = v_a[0:slab, 0 : X * part].astype(F32)
+        for j in range(Y - 1):
+            load_b = links.local(h_uy.at[j, q], v_b.at[pl.ds(0, slab), pl.ds(0, X * part)])
+            load_b.wait()
+            total = total + v_b[0:slab, 0 : X * part].astype(F32)
+        v_out[0:slab, 0 : X * part] = total.astype(BF)
+        store = links.local(
+            v_out.at[pl.ds(0, slab), pl.ds(0, X * part)],
+            h_us.at[q, pl.ds(pl.multiple_of(y * slab, slab), slab)],
+        )
+        store.wait()
+    own_rows = pl.ds(pl.multiple_of(y * slab, slab), slab)
+    gu_z = []
+    own_gu = []
+    for i in range(X):
+        span = pl.ds(i * part, part)
+        own_gu.append(
+            links.local(h_us.at[z, own_rows, span], gup_o.at[z * X + i, k, own_rows])
+        )
+        for a, t in to_z:
+            gu_z.append(
+                links.push(h_us.at[t, own_rows, span], gup_o.at[z * X + i, k, own_rows], a, t)
+            )
+
+    d_bias = v_vec[6:7, :].astype(F32)
+    wait_recvs(mlp_z)
+
+    def finish_result(span):
+        total = m_own[z, span, :].astype(F32)
+        for j in range(Z - 1):
+            total = total + m_zin[j, span, :].astype(F32)
+        row = lax.broadcasted_iota(jnp.int32, (step, 1), 0) + span.start + c * R
+        value = v_mid[span, :] + total + d_bias
+        m_kin[0, 0, span, :] = jnp.where(row < length, value, 0.0).astype(BF)
+
+    rows_loop(R, step, finish_result)
+    save_result = links.local(m_kin.at[0, 0], result_o)
+
+    gain_one = v_vec[0:1, :].astype(F32)
+    wait_recvs(g1_y)
+
+    def finish_input(span):
+        grad = v_g1k[0, y, span, :].astype(F32)
+        for j in range(Y - 1):
+            grad = grad + v_g1y[j, span, :].astype(F32)
+        values = v_rows[span, :].astype(F32)
+        center = values - jnp.mean(values, 1, keepdims=True)
+        rstd = lax.rsqrt(jnp.mean(center * center, 1, keepdims=True) + EPSILON)
+        hat = center * rstd
+        scaled = grad * gain_one
+        back = rstd * (
+            scaled
+            - jnp.mean(scaled, 1, keepdims=True)
+            - hat * jnp.mean(scaled * hat, 1, keepdims=True)
+        )
+        v_kin[0, 0, span, :] = (v_hat[span, :] + back).astype(BF)
+
+    rows_loop(R, step, finish_input)
+    save_input = links.local(v_kin.at[0, 0], igrad_o)
+
+    wait_recvs(gd_y)
+    add_blocks([gdown_o.at[k]] + [h_dy.at[j] for j in range(Y - 1)], h_ds, D)
+    links.sent(gd_y)
+    own_gd = links.local(h_ds, gdown_o.at[k])
+    gd_k = [links.push(h_ds, gdown_o.at[k], *to) for to in to_k]
+
+    def sum_z(own, extra, copies):
+        wait_recvs(copies)
+        total = own[0, z].astype(F32)
+        for j in range(Z - 1):
+            total = total + extra[j].astype(F32)
+        extra[0] = total.astype(extra.dtype)
+
+    block_c = pl.ds(pl.multiple_of(c * cols, cols), cols)
+
+    def cols_of(q):
+        return pl.ds(pl.multiple_of(q * cols, cols), cols)
+
+    sum_z(v_dwox, v_dwoz, do_z)
+    last = [links.local(v_dwoz.at[0], gwo_o.at[:, block_c])]
+    wo_y = [links.push(v_dwoz.at[0], gwo_o.at[:, block_c], *to) for to in to_y]
+    wo_k = [links.push(v_dwoz.at[0], gwo_o.at[:, block_c], *to) for to in to_k]
+
+    wait_all(own_gu)
+    wait_recvs(gu_z)
+    mine = gup_o.at[:, k, own_rows]
+    gu_y2 = [links.push(mine, mine, *to) for to in to_y]
+
+    sum_z(v_dwqx, v_dwqz, dq_z)
+    wide = pl.ds(0, cols)
+    tail = pl.ds(cols, 2 * HD)
+    last.append(links.local(v_dwqz.at[0, :, wide], gwq_o.at[:, block_c]))
+    last.append(links.local(v_dwqz.at[0, :, tail], gkv_o.at[c]))
+    wq_y = [links.push(v_dwqz.at[0, :, wide], gwq_o.at[:, block_c], *to) for to in to_y]
+    wq_k = [links.push(v_dwqz.at[0, :, wide], gwq_o.at[:, block_c], *to) for to in to_k]
+    kv_y = [links.push(v_dwqz.at[0, :, tail], gkv_o.at[c], *to) for to in to_y]
+    kv_k = [links.push(v_dwqz.at[0, :, tail], gkv_o.at[c], *to) for to in to_k]
+    sum_z(v_sgx, v_sgz, sg_z)
+    v_sga[c] = v_sgz[0]
+    sg_y = [links.push(v_sga.at[c], v_sga.at[c], *to) for to in to_y]
+    sg_k = [links.push(v_sga.at[c], v_sga.at[c], *to) for to in to_k]
+
+    for j in range(1, Y):
+        q = ys[j] * K + k
+        wo_y[j - 1].wait_recv()
+        wo_k += [links.push(gwo_o.at[:, cols_of(q)], gwo_o.at[:, cols_of(q)], *to) for to in to_k]
+        wq_y[j - 1].wait_recv()
+        wq_k += [links.push(gwq_o.at[:, cols_of(q)], gwq_o.at[:, cols_of(q)], *to) for to in to_k]
+        kv_y[j - 1].wait_recv()
+        kv_k += [links.push(gkv_o.at[q], gkv_o.at[q], *to) for to in to_k]
+        sg_y[j - 1].wait_recv()
+        sg_k += [links.push(v_sga.at[q], v_sga.at[q], *to) for to in to_k]
+    wait_recvs(gu_y2)
+    gu_k = [links.push(gup_o.at[:, k], gup_o.at[:, k], *to) for to in to_k]
+    wait_recvs(sg_k)
+    total = v_sga[0]
+    for q in range(1, C):
+        total = total + v_sga[q]
+    v_sgz[0] = total
+    last.append(links.local(v_sgz.at[0], small_o))
+    wait_recvs(gd_k + wo_k + wq_k + kv_k + gu_k)
+    wait_all(last + [own_gd, save_result, save_input])
+    links.drain()
+
+
+def backward_call(sizes, lengths, rows, gmlp, mid, seq, normed, qkv, att, wqkv, wo, vec, gub,
+                  g2part, mlppart, gdown, gup):
+    Y, K, Z, X = sizes
+    C, S = Y * K, Z * X
+    R, D = rows.shape
+    T = C * R
+    cols = D // C
+    qkv_cols = cols + 2 * HD
+    here = wqkv.shape[1]
+    part = gdown.shape[1]
+    half = min(part, here)
+    shape = jax.ShapeDtypeStruct
+    anywhere = pl.BlockSpec(memory_space=pl.ANY)
+    outs = [
+        shape((R, D), BF),
+        shape((R, D), BF),
+        shape((K, part, D), BF),
+        shape((S, K, here, part), BF),
+        shape((here, D), BF),
+        shape((here, D), BF),
+        shape((C, here, 2 * HD), BF),
+        shape((SMALL_ROWS, here), F32),
+        shape((X - 1, part, D), BF),
+        shape((Y - 1, part, D), BF),
+        shape((X - 1, Z, here, X * part), BF),
+        shape((Z, here, X * part), BF),
+        shape((Y - 1, Z, here // Y, X * part), BF),
+        shape((part, D), BF),
+    ]
+    return pl.pallas_call(
+        functools.partial(backward_kernel, sizes),
+        in_specs=[pl.BlockSpec(memory_space=pltpu.SMEM)] + [anywhere] * 15,
+        out_specs=[anywhere] * len(outs),
+        out_shape=outs,
+        scratch_shapes=[
+            pltpu.VMEM((Z, R, D), BF),
+            pltpu.VMEM((K - 1, Z, R, D), BF),
+            pltpu.VMEM((Z - 1, R, D), BF),
+            pltpu.VMEM((Z, R, D), BF),
+            pltpu.VMEM((K - 1, Z, R, D), BF),
+            pltpu.VMEM((Z - 1, R, D), BF),
+            pltpu.VMEM((R, D), BF),
+            pltpu.VMEM((R, D), BF),
+            pltpu.VMEM((R, D), F32),
+            pltpu.VMEM((R, D), F32),
+            pltpu.VMEM((SMALL_ROWS, D), BF),
+            pltpu.VMEM((C, R, cols), BF),
+            pltpu.VMEM((C, R, cols), BF),
+            pltpu.VMEM((S, here, cols), BF),
+            pltpu.VMEM((C, T, cols), BF),
+            pltpu.VMEM((K - 1, Y, T, cols), BF),
+            pltpu.VMEM((Y - 1, T, cols), BF),
+            pltpu.VMEM((T, cols), BF),
+            pltpu.VMEM((T, D), BF),
+            pltpu.VMEM((T, D), BF),
+            pltpu.VMEM((T, qkv_cols), BF),
+            pltpu.VMEM((T, qkv_cols), BF),
+            pltpu.VMEM((T, HD), F32),
+            pltpu.VMEM((T, HD), F32),
+            pltpu.VMEM((S, here, qkv_cols), BF),
+            pltpu.VMEM((Z, X, here, cols), BF),
+            pltpu.VMEM((X - 1, Z, here, cols), BF),
+            pltpu.VMEM((Z - 1, here, cols), BF),
+            pltpu.VMEM((Z, X, here, qkv_cols), BF),
+            pltpu.VMEM((X - 1, Z, here, qkv_cols), BF),
+            pltpu.VMEM((Z - 1, here, qkv_cols), BF),
+            pltpu.VMEM((K - 1, Y, R, D), BF),
+            pltpu.VMEM((Y - 1, R, D), BF),
+            pltpu.VMEM((T, HD), F32),
+            pltpu.VMEM((T, HD), F32),
+            pltpu.VMEM((SMALL_ROWS, D), F32),
+            pltpu.VMEM((Z, X, SMALL_ROWS, here), F32),
+            pltpu.VMEM((X - 1, Z, SMALL_ROWS, here), F32),
+            pltpu.VMEM((Z - 1, SMALL_ROWS, here), F32),
+            pltpu.VMEM((C, SMALL_ROWS, here), F32),
+            pltpu.VMEM((1, X * part), F32),
+            pltpu.VMEM((half, D), BF),
+            pltpu.VMEM((half, D), BF),
+            pltpu.VMEM((half, D), BF),
+            pltpu.SemaphoreType.DMA((sem_count(sizes),)),
+            pltpu.SemaphoreType.DMA((sem_count(sizes),)),
+            pltpu.SemaphoreType.DMA((64,)),
+        ],
+        compiler_params=pltpu.CompilerParams(
+            collective_id=2, has_side_effects=True, vmem_limit_bytes=62 * MIB
+        ),
+        name="layer_backward",
+    )(lengths, rows, gmlp, mid, seq, normed, qkv, att, wqkv, wo, vec, gub, g2part, mlppart, gdown, gup)
+
+
+def spread_kernel(src, dst):
+    dst[...] = src[0].astype(F32)
+
+
+def spread(blocks):
+    count, height, width = blocks.shape
+    return pl.pallas_call(
+        spread_kernel,
+        grid=(count,),
+        in_specs=[pl.BlockSpec((1, height, width), lambda i: (i, 0, 0))],
+        out_specs=pl.BlockSpec((height, width), lambda i: (0, i)),
+        out_shape=jax.ShapeDtypeStruct((height, count * width), F32),
+        name="spread",
+    )(blocks)
 
 
 def norm_parts(values):
@@ -656,23 +1333,14 @@
         up_weight,
         down_weight,
     )
-    wqkv = wqkv.reshape(D, qkv_cols)
-    wo = wo.reshape(D, cols)
     wup = wup.reshape(D, X * ff_part)
     wdown = wdown.reshape(X * ff_part, D)
     grad_mlp_all = grad_mlp_all.reshape(Z * K * R, D)
     normed_two_all = normed_two_all.reshape(Z * K * R, D)
-    queries, keys, values = qkv[:, :cols], qkv[:, cols : cols + HD], qkv[:, cols + HD :]
     top_logit = tops[:, :heads, 0].reshape(H)
-    gain_one = vectors[0].astype(F32)
-    gain_two = vectors[4].astype(F32)
-    d_bias = vectors[6].astype(F32)
     u_bias = vectors[8:12].reshape(K, 4 // K, Z, X, rows_here)
     u_bias_own = pick(pick(u_bias, k, 0), z, 1)
     u_bias_own = jnp.moveaxis(u_bias_own, 0, 1).reshape(-1).astype(F32)
-    rows_in = rows_low.astype(F32)
-    seq_hat, seq_rstd = norm_parts(seq_low.astype(F32))
-    hat_two, rstd_two = norm_parts(middle)
 
     pre_act = mm(normed_two_all, wup) + u_bias_own
     tanh = jnp.tanh(GELU_C * (pre_act + GELU_A * pre_act * pre_act * pre_act))
@@ -683,98 +1351,37 @@
     grad_act = mm_nt(grad_mlp_all, wdown)
     grad_pre_wide = grad_act * slope
     grad_pre = grad_pre_wide.astype(BF)
-    grad_two_part = mm_nt(grad_pre, wup).astype(BF)
-    grad_two = lax.psum_scatter(grad_two_part, ("z", "k"), tiled=True).astype(F32)
-    mlp_part = mm(act, wdown).astype(BF)
-    mlp_out = lax.psum_scatter(mlp_part, ("z", "k"), tiled=True).astype(F32)
-    result = (live_rows * (middle + mlp_out + d_bias)).astype(BF)[None]
-
-    grad_up_bias = jnp.sum(grad_pre.astype(F32), 0)
-    grad_down_bias = jnp.sum(grad_mlp.astype(F32), 0)
-
+    grad_two_part = mm_nt(grad_pre, wup).astype(BF).reshape(Z, K, R, D)
+    mlp_part = mm(act, wdown).astype(BF).reshape(Z, K, R, D)
+    grad_up_bias = jnp.sum(grad_pre.astype(F32), 0)[None, :]
     gdown = mm_tn(act, grad_mlp_all).astype(BF).reshape(X, ff_part, D)
-    gdown = sum_blocks(gdown, "x", X, 0)
-    gdown = sum_copies(gdown, "y", Y).astype(BF)
-    grad_down_weight = gather(gdown, "k", K, 0).reshape(ff_here, D).astype(F32)
-
-    gup = mm_tn(normed_two_all, grad_pre).astype(BF)
-    gup = gup.reshape(Z, X, Y, rows_here // Y, X * ff_part)
-    gup = sum_blocks(gup, "x", X, 1)
-    gup = sum_blocks(gup, "y", Y, 1).astype(BF)
-    gup = swap_blocks(gup, "z", Z, 0)
-    gup = gather(gather(gup, "y", Y, 0), "k", K, 1)
-    gup = gup.reshape(Y, K, Z, rows_here // Y, X, ff_part).transpose(0, 3, 2, 4, 1, 5)
-    grad_up_weight = gup.reshape(rows_here, FF).astype(F32)
-
-    grad_gain_two = jnp.sum(grad_two * hat_two, 0)
-    grad_shift_two = jnp.sum(grad_two, 0)
-    grad_middle = grad_out + norm_back(grad_two, gain_two, hat_two, rstd_two)
-    grad_branch = grad_middle.astype(BF)
-    grad_output_bias = jnp.sum(grad_branch.astype(F32), 0)
-    grad_branch_cols = swap_blocks(grad_branch.reshape(R, C, cols), ("y", "k"), C, 1)
-    grad_branch_cols = jnp.moveaxis(grad_branch_cols, 1, 0).reshape(T, cols)
-    grad_att = mm_nt(grad_branch_cols, wo).astype(BF).reshape(T, Y, K, cols)
-    grad_att = sum_blocks(grad_att, "k", K, 2)
-    grad_att = sum_blocks(grad_att, "y", Y, 1).astype(BF)
-    gout = mm_tn(attended_all, grad_branch_cols).astype(BF).reshape(Z, X, rows_here, cols)
-    gout = sum_blocks(gout, "x", X, 1).astype(BF)
-    gout = lax.psum_scatter(gout, "z")
-    gout = gather(gather(gout, "y", Y, 1), "k", K, 2)
-    grad_output_weight = gout.reshape(rows_here, D).astype(F32)
-
-    grad_queries, grad_keys, grad_values = attend_back(lengths, queries, keys, values, grad_att)
-    grad_qkv = jnp.concatenate([grad_queries, grad_keys.astype(BF), grad_values.astype(BF)], 1)
-    grad_one_part = mm_nt(grad_qkv, wqkv)
-    grad_gain_one = jnp.sum(grad_one_part * seq_hat, 0)
-    grad_shift_one = jnp.sum(grad_one_part, 0)
-    grad_one = grad_one_part.astype(BF).reshape(Y, K, R, D)
-    grad_one = sum_blocks(grad_one, "k", K, 1)
-    grad_one = sum_blocks(grad_one, "y", Y, 0)
-    hat_one, rstd_one = norm_parts(rows_in)
-    input_grad = (grad_middle + norm_back(grad_one, gain_one, hat_one, rstd_one)).astype(BF)[None]
-
-    gqkv = mm_tn(normed, grad_qkv).astype(BF).reshape(Z, X, rows_here, qkv_cols)
-    qkv_bias_grad = jnp.sum(grad_qkv.astype(F32), 0)
-    grad_query_bias = lax.dynamic_update_slice_in_dim(
-        jnp.zeros((D,), F32), qkv_bias_grad[:cols], c * cols, 0
+    gup = mm_tn(normed_two_all, grad_pre).astype(BF).reshape(Z, X, rows_here, X * ff_part)
+    backs = backward_call(
+        sizes,
+        lengths,
+        rows_low,
+        grad_mlp,
+        middle,
+        seq_low,
+        normed,
+        qkv,
+        attended_all,
+        wqkv,
+        wo,
+        vectors,
+        grad_up_bias,
+        grad_two_part,
+        mlp_part,
+        gdown,
+        gup,
     )
-    grad_up_bias_all = lax.dynamic_update_slice(
-        jnp.zeros((Z, X, K, ff_part), F32),
-        grad_up_bias.reshape(1, X, 1, ff_part),
-        (z, 0, k, 0),
-    ).reshape(S, ff_here)
-    small_grads = jnp.concatenate(
-        [
-            item.reshape(S, rows_here)
-            for item in (
-                grad_gain_one,
-                grad_shift_one,
-                grad_query_bias,
-                grad_output_bias,
-                grad_gain_two,
-                grad_shift_two,
-                grad_down_bias,
-            )
-        ]
-        + [grad_up_bias_all, qkv_bias_grad[cols + HD :].reshape(S, HD // S)],
-        1,
-    )
-    small_grads = jnp.pad(small_grads, ((0, 0), (0, small_rows * qkv_cols - small_len)))
-    small_grads = small_grads.astype(BF).reshape(Z, X, small_rows, qkv_cols)
-    gpacked = jnp.concatenate([gqkv, small_grads], 2)
-    gpacked = sum_blocks(gpacked, "x", X, 1).astype(BF)
-    gpacked = lax.psum_scatter(gpacked, "z")
-    gpacked = gather(gather(gpacked, "y", Y, 0), "k", K, 1).reshape(C, packed_rows, qkv_cols)
-    grad_query_weight = (
-        jnp.moveaxis(gpacked[:, :rows_here, :cols], 0, 1).reshape(rows_here, D).astype(F32)
-    )
-    grad_keyval_weight = jnp.sum(gpacked[:, :rows_here, cols:].astype(F32), 0)
-    small_sums = jnp.sum(gpacked[:, rows_here:].astype(F32), 0).reshape(-1)
-    place = 0
-    small_outs = []
-    for size in [rows_here] * 7 + [ff_here, HD // S]:
-        small_outs.append(small_sums[place : place + size])
-        place += size
+    result, input_grad, gdown, gup, gwo, gwq, gkv, small_sums = backs[:8]
+    grad_down_weight = gdown.reshape(ff_here, D).astype(F32)
+    grad_up_weight = spread(gup.reshape(S * K, rows_here, ff_part))
+    grad_output_weight = gwo.astype(F32)
+    grad_query_weight = gwq.astype(F32)
+    grad_keyval_weight = jnp.sum(gkv.astype(F32), 0)
+    grad_value_bias = lax.dynamic_slice_in_dim(small_sums[12], shard * (HD // S), HD // S, 0)
 
     factors = CLIP_LIMIT / jnp.maximum(top_logit, CLIP_LIMIT)
     column_scale = jnp.repeat(jnp.sqrt(factors), HD)
@@ -786,22 +1393,22 @@
     clipped_keyval_weight = (keyval_weight.astype(F32) * keyval_scale[None, :]).astype(BF)
 
     return (
-        result,
-        input_grad,
-        small_outs[0],
-        small_outs[1],
+        result[None],
+        input_grad[None],
+        small_sums[0],
+        small_sums[1],
         grad_query_weight,
-        small_outs[2],
+        small_sums[2],
         grad_keyval_weight,
-        small_outs[8],
+        grad_value_bias,
         grad_output_weight,
-        small_outs[3],
-        small_outs[4],
-        small_outs[5],
+        small_sums[3],
+        small_sums[4],
+        small_sums[5],
         grad_up_weight,
-        small_outs[7],
+        small_sums[8:12].reshape(-1),
         grad_down_weight,
-        small_outs[6],
+        small_sums[6],
         clipped_query_weight,
         clipped_query_bias,
         clipped_keyval_weight,

time: 642 us -> 514 us (0.80)
  Pallas kernels: 220 us -> 429 us
  waiting for transfers between devices: 170 us -> 0 us
  local copies, waits for them, and re-layouts: 83.4 us -> 10.4 us
  other arithmetic: 68.7 us -> 16.2 us
  starting transfers between devices: 16.1 us -> 0 us
  between operations: 16.6 us -> 2.15 us
  matrix products: 55.8 us -> 47.8 us
    pallas_call x1 -> x2, Pallas kernels: 5.71 us -> 256 us  [the longest x1 245 us: backward_call(): pl.pallas_call(functools.partial(backward_kernel, sizes), in_specs=[pl.Bl...]
    ppermute x23 -> x0, waiting for transfers between devices: 170 us -> none  [shift(): lax.ppermute(value, axis, [(i, (i + step) % count) for i in range(count)])]
    pallas_call x1, Pallas kernels: 214 us -> 174 us  [forward_call(): pl.pallas_call(functools.partial(forward_kernel, sizes), in_specs=[pl.Blo...]
    convert_element_type x9 -> x0, local copies, waits for them, and re-layouts: 37.3 us -> none  [the longest x2 25.1 us: body(): grad_up_weight = gup.reshape(rows_here, FF).astype(F32)]
    ppermute x23 -> x0, starting transfers between devices: 15.2 us -> none  [shift(): lax.ppermute(value, axis, [(i, (i + step) % count) for i in range(count)])]
    convert_element_type x12 -> x4, other arithmetic: 26.7 us -> 11.8 us  [the longest x1 6.66 us: body(): grad_down_weight = gdown.reshape(ff_here, D).astype(F32)]
    reduce_sum x13 -> x1, other arithmetic: 12.4 us -> 0.77 us  [body(): grad_keyval_weight = jnp.sum(gkv.astype(F32), 0)]
    another operation x13 -> x0, other arithmetic: 10.4 us -> none  [the longest x11 10.4 us: in_order(): jnp.stack([jnp.where(first, parts[0], parts[1]), jnp.where(first, parts[1...]
  transfers between devices with their start and end apart: 27 -> 0, of which waited for: 10 -> 0; matrix products, arithmetic and copies ran while one was open for 26% -> 0% of each run, Pallas kernels for 1% -> 0%
where the time goes in v2:
time: 514 us; the launch traced here: 506 us
  Pallas kernels  429 us (83%)
  matrix products  47.8 us (9%)
  other arithmetic  16.2 us (3%)
  local copies, waits for them, and re-layouts  10.4 us (2%)
    pallas_call x1, Pallas kernels, backward_call(): pl.pallas_call(functools.partial(backward_kernel, sizes), in_specs=[pl.Bl...  245 us
    pallas_call x1, Pallas kernels, forward_call(): pl.pallas_call(functools.partial(forward_kernel, sizes), in_specs=[pl.Blo...  174 us
    dot_general x2, matrix products, mm_nt(): lax.dot_general(left, right, (((1,), (1,)), ((), ())), preferred_element_...  18.2 us
    dot_general x2, matrix products, mm(): return jnp.dot(left, right, preferred_element_type=F32)  16.5 us
    dot_general x2, matrix products, mm_tn(): lax.dot_general(left, right, (((0,), (0,)), ((), ())), preferred_element_...  13.1 us
    pallas_call x1, Pallas kernels, spread(): pl.pallas_call(spread_kernel, grid=(count,), in_specs=[pl.BlockSpec((1, h...  10.9 us

profile of v2, /device:TPU:0, one launch (start us, length us, event | category | flops | bytes accessed | tf_op | source)
XLA Modules:
  0.0 506.0 jit_solution(3209045444236400022)
XLA Ops:
  1.3 2.0 fusion.7.gmlp
  3.3 0.7 tile.4
  4.1 0.7 reshape.154
  4.8 0.7 broadcast_in_dim.42
  5.4 0.7 broadcast_in_dim.43
  6.1 0.7 broadcast_in_dim.44
  6.7 0.7 broadcast_in_dim.45
  7.4 0.7 broadcast_in_dim.46
  8.1 0.7 broadcast_in_dim.47
  8.7 0.7 broadcast_in_dim.48
  9.4 0.6 pad_add_fusion.small
  10.0 173.7 %layer_forward.1 = (bf16[512,2048]{1,0:T(8,128)(2,1)}, bf16[8,256,768]{2,1,0:T(8,128)(2,1)}, bf16[8,256,512]{2,1,0:T(8,128)(2,1)}, bf16[8,256,1024]{2,1,0:T(8,12...) custom-call(s32[1]{0:T(128)} %copy.45.length_ref, ...), custom_call_target="tpu_custom_call" | custom-call | tf_op jit(solution)/shard_map/layer_forward/pallas_call | solution.py:588
  183.7 10.0 %fusion.10 = f32[1024,1024]{1,0:T(8,128)} fusion(bf16[1024,2048]{1,0:T(8,128)(2,1)} %bitcast.81, bf16[2048,1024]{1,0:T(8,128)(2,1)} %bitcast.75), kind=kOutput, calls=%fused_computation.39 | convolution fusion | flops 4294967296 | bytes 12582912 | tf_op jit(solution)/shard_map/dot_general | solution.py:25
  193.6 0.8 slice.33
  194.5 12.1 %convert_reduce_fusion = (f32[1024]{0:T(1024)}, bf16[1024,1024]{1,0:T(8,128)(2,1)S(1)}) fusion(f32[1024,1024]{1,0:T(8,128)} %fusion.10, f32[1024]{0:T(1024)S(1)} %bitcast.65, bf16[1024,2048]{1,0:T(8,128)(2,1)} %bitcast.79, bf16[1024,2048]{1,0:T(8,128)(2,1)} %bitcast.77), kind=kOutput, calls=%fused_computation.11 | convolution fusion | flops 4318034944 | bytes 14688256 | tf_op jit(solution)/shard_map/dot_general | solution.py:33
  206.6 6.2 %convolution_convert_fusion = bf16[2048,1024]{1,0:T(8,128)(2,1)} fusion(bf16[1024,2048]{1,0:T(8,128)(2,1)S(1)} %bitcast.82, bf16[1024,1024]{1,0:T(8,128)(2,1)S(1)} %get-tuple-element.72), kind=kOutput, calls=%fused_computation.12 | convolution fusion | flops 4297064448 | bytes 10485760 | tf_op jit(solution)/shard_map/dot_general | solution.py:29
  212.8 6.9 %convolution_convert_fusion.1 = bf16[1024,2048]{1,0:T(8,128)(2,1)} fusion(bf16[1024,2048]{1,0:T(8,128)(2,1)S(1)} %bitcast.80, f32[1024,1024]{1,0:T(8,128)S(1)} %copy-done.14, f32[1024]{0:T(1024)S(1)} %bitcast.66), kind=kOutput, calls=%fused_computation.13 | convolution fusion | flops 4307550208 | bytes 12587008 | tf_op jit(solution)/shard_map/dot_general | solution.py:29
  219.7 6.5 %convolution_convert_fusion.2 = bf16[1024,2048]{1,0:T(8,128)(2,1)} fusion(bf16[1024,2048]{1,0:T(8,128)(2,1)S(1)} %bitcast.78, f32[1024,1024]{1,0:T(8,128)S(1)} %copy-done.14, f32[1024]{0:T(1024)S(1)} %bitcast.67), kind=kOutput, calls=%fused_computation.14 | convolution fusion | flops 4307550208 | bytes 12587008 | tf_op jit(solution)/shard_map/dot_general | solution.py:25
  226.3 6.1 %convolution_convert_fusion.3 = bf16[1024,2048]{1,0:T(8,128)(2,1)} fusion(bf16[1024,1024]{1,0:T(8,128)(2,1)S(1)} %get-tuple-element.72, bf16[2048,1024]{1,0:T(8,128)(2,1)S(1)} %bitcast.76), kind=kOutput, calls=%fused_computation.15 | convolution fusion | flops 4297064448 | bytes 10485760 | tf_op jit(solution)/shard_map/dot_general | solution.py:33
  232.3 244.8 %layer_backward.1 = (bf16[128,2048]{1,0:T(8,128)(2,1)}, bf16[128,2048]{1,0:T(8,128)(2,1)}, bf16[2,512,2048]{2,1,0:T(8,128)(2,1)}, bf16[8,2,256,512]{3,2,1,0:T(8,...) custom-call(s32[1]{0:T(128)} %copy.45.length_ref, ...), custom_call_target="tpu_custom_call" | custom-call | tf_op jit(solution)/shard_map/layer_backward/pallas_call | solution.py:1164
  477.1 6.7 %bitcast_convert_fusion = f32[1024,2048]{1,0:T(8,128)} fusion(bf16[2,512,2048]{2,1,0:T(8,128)(2,1)} %get-tuple-element.59), kind=kLoop, calls=%fused_computation.9 | loop fusion | flops 2097152 | bytes 12582912 | tf_op jit(solution)/shard_map/convert_element_type | solution.py:1379
  483.8 10.9 %spread.1 = f32[256,8192]{1,0:T(8,128)} custom-call(bf16[16,256,512]{2,1,0:T(8,128)(2,1)} %bitcast.58), custom_call_target="tpu_custom_call" | custom-call | tf_op jit(solution)/shard_map/spread/pallas_call | solution.py:1231
  494.8 1.6 convert_element_type.121
  496.3 1.6 convert_element_type.123
  497.9 0.8 convert_reduce_fusion.1
  498.6 0.6 fusion.9
  499.8 0.6 copy.39
  500.4 0.6 fusion.8
  501.8 1.2 multiply_convert_fusion.1
  503.7 0.7 multiply_convert_fusion.2
  504.4 0.8 copy.46
  505.2 0.8 copy.47
  (44 shorter events, 1.5 us)
Async XLA Ops:
  194.5 12.1 %copy-start.13 = (bf16[4,2,128,2048]{3,2,1,0:T(8,128)(2,1)S(1)}, bf16[4,2,128,2048]{3,2,1,0:T(8,128)(2,1)}, u32[]{:S(2)}) copy-start(bf16[4,2,128,2048]{3,2,1,0:T(8,128)(2,1)} %get-tuple-element.50) | copy-start | bytes 12582916
  206.6 6.2 %copy-start.12 = (bf16[4,2,128,2048]{3,2,1,0:T(8,128)(2,1)S(1)}, bf16[4,2,128,2048]{3,2,1,0:T(8,128)(2,1)}, u32[]{:S(2)}) copy-start(bf16[4,2,128,2048]{3,2,1,0:T(8,128)(2,1)} %get-tuple-element.48) | copy-start | bytes 12582916
  206.6 6.2 %copy-start.14 = (f32[1024,1024]{1,0:T(8,128)S(1)}, f32[1024,1024]{1,0:T(8,128)}, u32[]{:S(2)}) copy-start(f32[1024,1024]{1,0:T(8,128)} %fusion.10) | copy-start | bytes 12582916
  212.8 6.9 %copy-start.11 = (bf16[2,512,2048]{2,1,0:T(8,128)(2,1)S(1)}, bf16[2,512,2048]{2,1,0:T(8,128)(2,1)}, u32[]{:S(2)}) copy-start(bf16[2,512,2048]{2,1,0:T(8,128)(2,1)} %get-tuple-element.49) | copy-start | bytes 12582916
  219.7 6.6 %copy-start.10 = (bf16[8,256,1024]{2,1,0:T(8,128)(2,1)S(1)}, bf16[8,256,1024]{2,1,0:T(8,128)(2,1)}, u32[]{:S(2)}) copy-start(bf16[8,256,1024]{2,1,0:T(8,128)(2,1)} %get-tuple-element.51) | copy-start | bytes 12582916
  483.8 10.9 %copy-start.2 = (bf16[256,2048]{1,0:T(8,128)(2,1)S(1)}, bf16[256,2048]{1,0:T(8,128)(2,1)}, u32[]{:S(2)}) copy-start(bf16[256,2048]{1,0:T(8,128)(2,1)} %get-tuple-element.55) | copy-start | bytes 3145732
  483.8 12.5 %copy-start.1 = (bf16[256,2048]{1,0:T(8,128)(2,1)S(1)}, bf16[256,2048]{1,0:T(8,128)(2,1)}, u32[]{:S(2)}) copy-start(bf16[256,2048]{1,0:T(8,128)(2,1)} %get-tuple-element.57) | copy-start | bytes 3145732
  494.7 3.2 copy-start.4
  494.7 3.9 copy-start.7
  494.7 5.7 %copy-start.8 = (f32[4,8,128]{2,1,0:T(8,128)S(1)}, f32[4,8,128]{2,1,0:T(8,128)}, u32[]{:S(2)}) copy-start(f32[4,8,128]{2,1,0:T(8,128)} %get-tuple-element.60) | copy-start | bytes 49156
  494.7 6.5 %copy-start.9 = (bf16[256]{0:T(256)(128)(2,1)S(1)}, bf16[256]{0:T(256)(128)(2,1)}, u32[]{:S(2)}) copy-start(bf16[256]{0:T(256)(128)(2,1)} %param.22) | copy-start | bytes 1540
  494.7 7.1 %copy-start = (bf16[256,2048]{1,0:T(8,128)(2,1)S(1)}, bf16[256,2048]{1,0:T(8,128)(2,1)}, u32[]{:S(2)}) copy-start(bf16[256,2048]{1,0:T(8,128)(2,1)} %wq.1) | copy-start | bytes 3145732
  494.7 9.0 %copy-start.3 = (bf16[256,256]{1,0:T(8,128)(2,1)S(1)}, bf16[256,256]{1,0:T(8,128)(2,1)}, u32[]{:S(2)}) copy-start(bf16[256,256]{1,0:T(8,128)(2,1)} %wkv.1) | copy-start | bytes 393220
  496.3 8.1 %copy-start.6 = (bf16[128,2048]{1,0:T(8,128)(2,1)S(1)}, bf16[128,2048]{1,0:T(8,128)(2,1)}, u32[]{:S(2)}) copy-start(bf16[128,2048]{1,0:T(8,128)(2,1)} %get-tuple-element.52) | copy-start | bytes 1572868
  496.3 8.9 %copy-start.5 = (bf16[128,2048]{1,0:T(8,128)(2,1)S(1)}, bf16[128,2048]{1,0:T(8,128)(2,1)}, u32[]{:S(2)}) copy-start(bf16[128,2048]{1,0:T(8,128)(2,1)} %get-tuple-element.53) | copy-start | bytes 1572868
